TPU v7x, 32 devices: a whole 2x2x4 slice. The times are simulated.
32 devices in a mesh: ch: 4 (over z), ha: 2 (over x), dp: 4 (over y, core).
Axes of the slice: x: 2, y: 2, z: 4, core: 2. Of those that a mesh axis runs over, the one named last changes fastest.
Arguments:
- features: bfloat16 [384, 4, 4, 4, 128], P('ch', 'dp', None, 'ha'), may hold values from -26 to 26
- frame_count: int32 [4], P('dp'), may hold values from 1 to 4, as said below
- norm1_gain: float32 [384], P('ch'), may hold values from 0.5 to 2
- norm1_shift: float32 [384], P('ch'), may hold values from -3 to 3
- qkv_weight: bfloat16 [384, 1152], replicated, may hold values from -0.51031036 to 0.51031036
- qkv_bias: float32 [1152], replicated, may hold values from -3 to 3
- out_weight: bfloat16 [384, 384], replicated, may hold values from -0.3125 to 0.3125
- out_bias: float32 [384], replicated, may hold values from -3 to 3
- norm2_gain: float32 [384], P('ch'), may hold values from 0.5 to 2
- norm2_shift: float32 [384], P('ch'), may hold values from -3 to 3
- conv_weight: bfloat16 [3, 3, 3, 384, 384], P(None, None, None, 'ch'), may hold values from -0.0625 to 0.0625
- conv_bias: float32 [384], P('ch'), may hold values from -3 to 3
- cotangent: bfloat16 [384, 4, 4, 4, 128], P('ch', 'dp', None, 'ha'), may hold values from -0.0625 to 0.0625
Outputs:
- mixed: bfloat16 [384, 4, 4, 4, 128], P('ch', 'dp', None, 'ha')
- weight_grad: float32 [3, 3, 3, 384, 384], P(None, None, None, 'ch')
Inputs may be any that keep to these rules, and one draw needn't show every extreme that they name: `frame_count`: some clip has all 4 frames valid and some clip only one.
All inputs are finite; a program needn't handle non-finite values.
Results may differ from a plain program's by a relative error of at most 0.015.
Values may be sent and summed in bfloat16 or wider, within the bound.
A program may use at most 64 MiB of HBM per device.

v0:
```python
import jax
import jax.numpy as jnp
from jax import lax
from jax.sharding import PartitionSpec as P

GROUPS = 32


EPS = 1e-06


def padded_2(x, sides, width):
    for axis, dim in sides:
        count, length = (lax.axis_size(axis), x.shape[dim])
        up = [(i, (i + 1) % count) for i in range(count - 1)]
        down = [(j, i) for i, j in up]
        last = lax.slice_in_dim(x, length - width, length, axis=dim)
        leading = lax.slice_in_dim(x, 0, width, axis=dim)
        before = lax.ppermute(last, axis, up)
        after = lax.ppermute(leading, axis, down)
        x = jnp.concatenate([before, x, after], axis=dim)
    return x


def frame_mask(frame_count, frames):
    position = lax.broadcasted_iota(jnp.int32, (frame_count.shape[0], frames), 1)
    return (position < frame_count[:, None]).astype(jnp.float32)


def moments(values, mask, groups):
    chans, clips, frames, rows, cols = values.shape
    data = values.astype(jnp.float32).reshape(groups, chans // groups, clips, frames, rows * cols)
    first = jnp.einsum("gkbfp,bf->gb", data, mask)
    second = jnp.einsum("gkbfp,bf->gb", data * data, mask)
    return (first, second)


def normalize(values, first, second, count, gain, shift, groups):
    chans, clips, frames, rows, cols = values.shape
    mean = first / count[None, :]
    var = second / count[None, :] - mean * mean
    scale = lax.rsqrt(var + EPS)
    data = values.astype(jnp.float32).reshape(groups, chans // groups, clips, frames, rows * cols)
    normed = (data - mean[:, None, :, None, None]) * scale[:, None, :, None, None]
    normed = normed.reshape(values.shape)
    return normed * gain[:, None, None, None, None] + shift[:, None, None, None, None]


def attend(carry, queries, keys, values, scale):
    top, total, acc = carry
    scores = jnp.einsum("itc,isc->its", queries, keys, preferred_element_type=jnp.float32) * scale
    new_top = jnp.max(scores, axis=2)
    factor = jnp.exp(top - new_top)
    weights = jnp.exp(scores - new_top[..., None])
    total = total * factor + jnp.sum(weights, axis=2)
    acc = acc * factor[..., None] + jnp.einsum(
        "its,isc->itc", weights.astype(jnp.bfloat16), values, preferred_element_type=jnp.float32
    )
    return (new_top, total, acc)


def tap_stack(padded, time_tap, frames, rows, cols):
    windows = []
    for row_tap in range(3):
        for col_tap in range(3):
            windows.append(
                padded[
                    :,
                    :,
                    time_tap : time_tap + frames,
                    row_tap : row_tap + rows,
                    col_tap : col_tap + cols,
                ]
            )
    return jnp.concatenate(windows, axis=0)


def body(
    features,
    frame_count,
    norm1_gain,
    norm1_shift,
    qkv_weight,
    qkv_bias,
    out_weight,
    out_bias,
    norm2_gain,
    norm2_shift,
    conv_weight,
    conv_bias,
    cotangent,
):
    chans, clips, frames, rows, cols = features.shape
    groups = GROUPS // lax.axis_size("ch")
    mask = frame_mask(frame_count, frames)
    count = frame_count.astype(jnp.float32) * (chans // groups * rows * lax.axis_size("ha") * cols)
    first, second = moments(features, mask, groups)
    first, second = lax.psum((first, second), "ha")
    normed = normalize(features, first, second, count, norm1_gain, norm1_shift, groups).astype(
        jnp.bfloat16
    )
    by_frame = lax.all_to_all(normed, "ch", split_axis=2, concat_axis=0, tiled=True)
    width = by_frame.shape[0]
    items = clips * by_frame.shape[2]
    tok_rows = rows * cols
    tokens = by_frame.reshape(width, items, tok_rows)
    queries = lax.dot_general(
        tokens, qkv_weight[:, :width], (((0,), (0,)), ((), ())), preferred_element_type=jnp.float32
    )
    queries = (queries + qkv_bias[:width]).astype(jnp.bfloat16)
    scale = width ** (-0.5)
    start_carry = (
        jnp.full((items, tok_rows), -jnp.inf, jnp.float32),
        jnp.zeros((items, tok_rows), jnp.float32),
        jnp.zeros((items, tok_rows, width), jnp.float32),
    )
    pairs = lax.dot_general(
        tokens, qkv_weight[:, width:], (((0,), (0,)), ((), ())), preferred_element_type=jnp.float32
    )
    pairs = (pairs + qkv_bias[width:]).astype(jnp.bfloat16)
    piece = lax.all_gather(pairs, "ha", axis=1, tiled=True)
    top, total, acc = attend(start_carry, queries, piece[..., :width], piece[..., width:], scale)
    attended = (acc / total[..., None]).astype(jnp.bfloat16)
    projected = lax.dot_general(
        out_weight, attended, (((0,), (2,)), ((), ())), preferred_element_type=jnp.float32
    )
    projected = (projected + out_bias[:, None, None]).astype(jnp.bfloat16).reshape(by_frame.shape)
    update = lax.all_to_all(projected, "ch", split_axis=0, concat_axis=2, tiled=True)
    hidden = (features.astype(jnp.float32) + update.astype(jnp.float32)).astype(jnp.bfloat16)
    first, second = moments(hidden, mask, groups)
    first, second = lax.psum((first, second), "ha")
    gated = jax.nn.silu(
        normalize(hidden, first, second, count, norm2_gain, norm2_shift, groups)
    ).astype(jnp.bfloat16)
    with_rows = padded_2(gated, (("ha", 3),), 1)
    padded = jnp.pad(with_rows, ((0, 0), (0, 0), (2, 0), (0, 0), (1, 1)))
    stacks = [tap_stack(padded, time_tap, frames, rows, cols) for time_tap in range(3)]
    amount = chans * lax.axis_size("ch")
    summed = jnp.zeros((amount, clips, frames, rows, cols), jnp.float32)
    for time_tap in range(3):
        part = conv_weight[time_tap].reshape(9 * chans, amount)
        summed = summed + lax.dot_general(
            part, stacks[time_tap], (((0,), (0,)), ((), ())), preferred_element_type=jnp.float32
        )
    conv_out = lax.psum_scatter(
        summed.astype(jnp.bfloat16), "ch", scatter_dimension=0, tiled=True
    ).astype(jnp.float32)
    mixed = mask[None, :, :, None, None] * (
        hidden.astype(jnp.float32) + conv_out + conv_bias[:, None, None, None, None]
    )
    mixed = mixed.astype(jnp.bfloat16)
    masked_cot = cotangent * mask.astype(jnp.bfloat16)[None, :, :, None, None]
    full_width = chans * lax.axis_size("ch")
    carry = jnp.zeros((3, 9 * chans, full_width), jnp.float32)
    piece = lax.all_gather(masked_cot, "ch", axis=0, tiled=True)
    start = jnp.int32(0)
    for time_tap in range(3):
        part = lax.dot_general(
            stacks[time_tap],
            piece,
            (((1, 2, 3, 4), (1, 2, 3, 4)), ((), ())),
            preferred_element_type=jnp.float32,
        )
        carry = lax.dynamic_update_slice(
            carry, part[None], (jnp.int32(time_tap), jnp.int32(0), start)
        )
    grad_table = carry
    grad_table = grad_table.reshape(3, 3, 3, chans, full_width)
    weight_grad = lax.psum(grad_table, ("ha", "dp"))
    return (mixed, weight_grad)


def solution(mesh):
    placed = (
        P("ch", "dp", None, "ha", None),
        P("dp"),
        P("ch"),
        P("ch"),
        P(),
        P(),
        P(),
        P(),
        P("ch"),
        P("ch"),
        P(None, None, None, "ch", None),
        P("ch"),
        P("ch", "dp", None, "ha", None),
    )
    return jax.shard_map(
        body,
        mesh=mesh,
        in_specs=placed,
        out_specs=(P("ch", "dp", None, "ha", None), P(None, None, None, "ch", None)),
        check_vma=False,
    )
```

profile of v0, /device:TPU:0, one launch (start us, length us, event | category | flops | bytes accessed | tf_op | source)
XLA Modules:
  0.0 198.0 jit_solution(10997418595436640194)
XLA Ops:
  8.0 1.2 fusion.57
  10.4 5.9 %all-reduce.3 = (f32[8,1]{0,1:T(1,128)S(1)}, f32[8,1]{0,1:T(1,128)S(1)}) all-reduce(f32[8,1]{0,1:T(1,128)S(1)} %convolution_bitcast_fusion.3, f32[8,1]{0,1:T(1,128)S(1)} %convolution_bitcast_fusion.2), channel_id=1, replica_groups=mesh['ch'=4,'ha'=2,'dp'=4] {'ha'}, use_global_device_ids=true, to_apply=%region_2.0 | all-reduce | flops 16 | bytes 128 | tf_op jit(solution)/shard_map/psum | solution.py:98
  16.6 1.8 fusion.78
  18.4 5.5 %all-to-all-start = ((bf16[96,1,4,2,128]{4,0,3,1,2:T(8,128)(2,1)}), bf16[96,1,4,2,128]{4,0,3,1,2:T(8,128)(2,1)S(1)}, u32[]{:S(2)}, u32[]{:S(2)}) async-start(bf16[96,1,4,2,128]{4,0,3,1,2:T(8,128)(2,1)} %fusion.78), calls=%async_computation | async-start | bytes 393216 | tf_op jit(solution)/shard_map/all_to_all | solution.py:102
  24.0 0.7 slice.120
  24.7 5.5 %all-to-all-done = bf16[96,1,4,2,128]{4,0,3,1,2:T(8,128)(2,1)S(1)} async-done(((bf16[96,1,4,2,128]{4,0,3,1,2:T(8,128)(2,1)}), bf16[96,1,4,2,128]{4,0,3,1,2:T(8,128)(2,1)S(1)}, u32[]{:S(2)}, u32[]{:S(2)}) %all-to-all-start) | async-done | bytes 196640 | tf_op jit(solution)/shard_map/all_to_all | solution.py:102
  30.4 1.5 fusion.37
  31.8 8.9 %all-gather = bf16[512,768]{1,0:T(8,128)(2,1)S(1)} all-gather(bf16[256,768]{1,0:T(8,128)(2,1)S(1)} %fusion.37), channel_id=2, replica_groups=mesh['ch'=4,'ha'=2,'dp'=4] {'ha'}, dimensions={0}, use_global_device_ids=true | all-gather | bytes 1179648 | tf_op jit(solution)/shard_map/all_gather | solution.py:121
  40.8 1.6 fusion.104
  42.7 0.6 fusion.46
  43.5 10.0 %all_to_all.24 = bf16[384,1,1,2,128]{4,3,2,1,0:T(2,128)(2,1)S(1)} all-to-all(bf16[384,1,1,2,128]{4,3,2,1,0:T(2,128)(2,1)S(1)} %copy.33), channel_id=1, replica_groups=mesh['ch'=4,'ha'=2,'dp'=4] {'ch'}, dimensions={0} | all-to-all | bytes 393216 | tf_op jit(solution)/shard_map/all_to_all | solution.py:128
  54.3 5.0 %all-reduce.2 = (f32[8,1]{0,1:T(1,128)S(1)}, f32[8,1]{0,1:T(1,128)S(1)}) all-reduce(f32[8,1]{0,1:T(1,128)S(1)} %convolution_bitcast_fusion.1, f32[8,1]{0,1:T(1,128)S(1)} %convolution_bitcast_fusion), channel_id=1, replica_groups=mesh['ch'=4,'ha'=2,'dp'=4] {'ha'}, use_global_device_ids=true, to_apply=%region_10.11 | all-reduce | flops 16 | bytes 128 | tf_op jit(solution)/shard_map/psum | solution.py:131
  60.0 1.3 collective-permute-start.1
  61.3 4.6 %collective-permute-start = (bf16[96,1,4,1,128]{4,0,3,2,1:T(8,128)(2,1)S(1)}, bf16[96,1,4,1,128]{4,0,3,2,1:T(8,128)(2,1)S(1)}, u32[]{:S(2)}, u32[]{:S(2)}) collective-permute-start(bf16[96,1,4,1,128]{4,0,3,2,1:T(8,128)(2,1)S(1)} %get-tuple-element.47), channel_id=1, source_target_pairs={{0,4},{1,5},{2,6},{3,7},{8,12},{9,13},{10,14},{11,15},{16,20},{17,... | collective-permute-start | bytes 294920 | tf_op jit(solution)/shard_map/ppermute | solution.py:19
  66.0 0.4 collective-permute-done.1
  66.5 1.5 collective-permute-done
  68.0 0.4 fusion.41
  69.8 0.4 constant_dynamic-update-slice_fusion
  71.0 1.0 fusion.15
  72.1 0.6 copy-done.4
  72.6 1.0 fusion.11
  73.7 1.9 fusion.34
  75.8 21.4 %all_gather.7 = bf16[384,1,4,2,128]{4,0,3,2,1:T(8,128)(2,1)S(1)} all-gather(bf16[96,1,4,2,128]{4,0,3,2,1:T(8,128)(2,1)S(1)} %copy_multiply_fusion), channel_id=1, replica_groups=mesh['ch'=4,'ha'=2,'dp'=4] {'ch'}, dimensions={0}, use_global_device_ids=true | all-gather | bytes 983040 | tf_op jit(solution)/shard_map/all_gather | solution.py:155
  97.2 2.6 %fusion.19 = f32[1,864,384]{2,1,0:T(8,128)S(1)} fusion(bf16[864,1,4,2,128]{4,0,3,2,1:T(8,128)(2,1)} %copy-done.6, bf16[384,1,4,2,128]{4,0,3,2,1:T(8,128)(2,1)S(1)} %all_gather.7), kind=kOutput, calls=%fused_computation.21 | convolution fusion | flops 679477248 | bytes 3883008 | tf_op jit(solution)/shard_map/dot_general | solution.py:158
  99.8 2.2 %dynamic_update_slice.9 = f32[3,864,384]{2,1,0:T(8,128)} pad(f32[1,864,384]{2,1,0:T(8,128)S(1)} %fusion.19, f32[]{:T(128)} %constant.11.clone.1), padding=0_2x0_0x0_0 | pad | bytes 5308420 | tf_op jit(solution)/shard_map/dynamic_update_slice | solution.py:164
  102.0 2.2 %fusion.25 = f32[3,864,384]{2,1,0:T(8,128)} fusion(f32[3,864,384]{2,1,0:T(8,128)} %dynamic_update_slice.9, bf16[864,1,4,2,128]{4,0,3,2,1:T(8,128)(2,1)S(1)} %copy-done.5, bf16[384,1,4,2,128]{4,0,3,2,1:T(8,128)(2,1)S(1)} %all_gather.7), kind=kOutput, calls=%fused_computation.23 | convolution fusion | flops 679477248 | bytes 3883008 | tf_op jit(solution)/shard_map/dot_general | solution.py:158
  104.1 2.2 %fusion.31 = f32[3,864,384]{2,1,0:T(8,128)} fusion(f32[3,864,384]{2,1,0:T(8,128)} %fusion.25, bf16[864,1,4,2,128]{4,0,3,2,1:T(8,128)(2,1)S(1)} %slice_dynamic-update-slice_fusion, bf16[384,1,4,2,128]{4,0,3,2,1:T(8,128)(2,1)S(1)} %all_gather.7), kind=kOutput, calls=%fused_computation.25 | convolution fusion | flops 679477248 | bytes 3883008 | tf_op jit(solution)/shard_map/dot_general | solution.py:158
  106.4 0.6 copy-done.9
  107.0 1.1 fusion.71
  108.0 0.8 copy.40
  108.8 77.4 %all-reduce.6.cloned.1.call-done = f32[3,3,3,96,384]{4,3,2,1,0:T(8,128)} async-done(((f32[3,3,3,96,384]{4,3,2,1,0:T(8,128)}), f32[3,3,3,96,384]{4,3,2,1,0:T(8,128)}) %all-reduce.6.cloned.1.call-update) | async-done | bytes 3981328 | tf_op jit(solution)/shard_map/psum | solution.py:169
  186.3 4.3 %copy.98 = f32[3,3,3,96,384]{4,3,2,1,0:T(8,128)} copy(f32[3,3,3,96,384]{4,3,2,1,0:T(8,128)} %all-reduce.6.cloned.1.call-done) | data formatting | bytes 7962624
  (73 shorter events, 5.5 us)
Async XLA Ops:
  8.0 34.6 %copy-start = (bf16[384,384]{1,0:T(8,128)(2,1)S(1)}, bf16[384,384]{1,0:T(8,128)(2,1)}, u32[]{:S(2)}) copy-start(bf16[384,384]{1,0:T(8,128)(2,1)} %param.19) | copy-start | bytes 884740
  18.4 22.4 %slice-start = ((f32[1152]{0:T(1024)}), f32[384]{0:T(512)S(1)}, s32[]{:S(2)}) async-start(f32[1152]{0:T(1024)} %param.18), calls=%async_computation.5 | async-start | bytes 4096 | tf_op jit(solution)/shard_map/slice | solution.py:110
  18.4 11.8 %all-to-all-start = ((bf16[96,1,4,2,128]{4,0,3,1,2:T(8,128)(2,1)}), bf16[96,1,4,2,128]{4,0,3,1,2:T(8,128)(2,1)S(1)}, u32[]{:S(2)}, u32[]{:S(2)}) async-start(bf16[96,1,4,2,128]{4,0,3,1,2:T(8,128)(2,1)} %fusion.78), calls=%async_computation | async-start | bytes 393216 | tf_op jit(solution)/shard_map/all_to_all | solution.py:102
  24.0 82.4 %reduce-scatter.2.cloned.1.call-start = ((), (), s32[]{:S(2)}) async-start(), calls=%async_computation.3 | async-start | bytes 983040 | tf_op jit(solution)/shard_map/reduce_scatter | solution.py:145
  31.8 10.8 %copy-start.10 = (f32[384]{0:T(512)S(1)}, f32[384]{0:T(512)}, u32[]{:S(2)}) copy-start(f32[384]{0:T(512)} %param.20) | copy-start | bytes 4612
  42.6 10.8 %copy-start.2 = (bf16[96,1,4,2,128]{4,3,2,1,0:T(2,128)(2,1)S(1)}, bf16[96,1,4,2,128]{4,3,2,1,0:T(2,128)(2,1)}, u32[]{:S(2)}) copy-start(bf16[96,1,4,2,128]{4,3,2,1,0:T(2,128)(2,1)} %param.13) | copy-start | bytes 589828
  42.7 16.9 %copy-start.7 = (f32[96]{0:T(128)S(1)}, f32[96]{0:T(128)}, u32[]{:S(2)}) copy-start(f32[96]{0:T(128)} %param.22) | copy-start | bytes 1156
  42.7 16.9 %copy-start.8 = (f32[96]{0:T(128)S(1)}, f32[96]{0:T(128)}, u32[]{:S(2)}) copy-start(f32[96]{0:T(128)} %param.21) | copy-start | bytes 1156
  43.3 22.6 %copy-start.1 = (bf16[3,3,3,96,384]{4,3,2,1,0:T(8,128)(2,1)S(1)}, bf16[3,3,3,96,384]{4,3,2,1,0:T(8,128)(2,1)}, u32[]{:S(2)}) copy-start(bf16[3,3,3,96,384]{4,3,2,1,0:T(8,128)(2,1)} %param.23) | copy-start | bytes 5971972
  60.0 6.5 %collective-permute-start.1 = (bf16[96,1,4,1,128]{4,0,3,2,1:T(8,128)(2,1)S(1)}, bf16[96,1,4,1,128]{4,0,3,2,1:T(8,128)(2,1)S(1)}, u32[]{:S(2)}, u32[]{:S(2)}) collective-permute-start(bf16[96,1,4,1,128]{4,0,3,2,1:T(8,128)(2,1)S(1)} %get-tuple-element.48), channel_id=1, source_target_pairs={{4,0},{5,1},{6,2},{7,3},{12,8},{13,9},{14,10},{15,11},{20,16},{21,... | collective-permute-start | bytes 294920 | tf_op jit(solution)/shard_map/ppermute | solution.py:20
  61.3 6.8 %collective-permute-start = (bf16[96,1,4,1,128]{4,0,3,2,1:T(8,128)(2,1)S(1)}, bf16[96,1,4,1,128]{4,0,3,2,1:T(8,128)(2,1)S(1)}, u32[]{:S(2)}, u32[]{:S(2)}) collective-permute-start(bf16[96,1,4,1,128]{4,0,3,2,1:T(8,128)(2,1)S(1)} %get-tuple-element.47), channel_id=1, source_target_pairs={{0,4},{1,5},{2,6},{3,7},{8,12},{9,13},{10,14},{11,15},{16,20},{17,... | collective-permute-start | bytes 294920 | tf_op jit(solution)/shard_map/ppermute | solution.py:19
  70.8 1.2 copy-start.6
  70.8 1.8 copy-start.4
  73.7 2.0 %copy-start.3 = (bf16[96,1,4,2,128]{4,3,2,1,0:T(2,128)(2,1)S(1)}, bf16[96,1,4,2,128]{4,3,2,1,0:T(2,128)(2,1)}, u32[]{:S(2)}) copy-start(bf16[96,1,4,2,128]{4,3,2,1,0:T(2,128)(2,1)} %param.25) | copy-start | bytes 589828
  75.6 110.7 %all-reduce.6.cloned.1.call-start = ((), (), s32[]{:S(2)}) async-start(), calls=%async_computation.4 | async-start | bytes 7962624 | tf_op jit(solution)/shard_map/psum | solution.py:169
  99.8 2.2 %copy-start.5 = (bf16[864,1,4,2,128]{4,0,3,2,1:T(8,128)(2,1)S(1)}, bf16[864,1,4,2,128]{4,0,3,2,1:T(8,128)(2,1)}, u32[]{:S(2)}) copy-start(bf16[864,1,4,2,128]{4,0,3,2,1:T(8,128)(2,1)} %copy-done.4) | copy-start | bytes 5308420
  106.3 0.7 copy-start.9
Sparse Core Ops, SparseCore 0:
  75.7 27.0 reduce-scatter.1
Sparse Core Ops, SparseCore 1:
  106.4 79.8 all-reduce.5
where the time goes:
time: 199 us; the launch traced here: 198 us
  waiting for transfers between devices  85 us (43%)
  blocking collectives  51.1 us (26%)
  between operations  16.5 us (8%)
  matrix products  15 us (8%)
  local copies, waits for them, and re-layouts  12.8 us (6%)
  starting transfers between devices  11.4 us (6%)
  other arithmetic  6.16 us (3%)
    psum x1, waiting for transfers between devices, body(): weight_grad = lax.psum(grad_table, ('ha', 'dp'))  77.4 us
    all_gather x1, blocking collectives, body(): piece = lax.all_gather(masked_cot, 'ch', axis=0, tiled=True)  21.4 us
    psum x2, blocking collectives, body(): first, second = lax.psum((first, second), 'ha')  10.8 us
    all_to_all x1, blocking collectives, body(): lax.all_to_all(projected, 'ch', split_axis=0, concat_axis=2, tiled=True)  9.99 us
    all_gather x1, blocking collectives, body(): piece = lax.all_gather(pairs, 'ha', axis=1, tiled=True)  8.94 us
    unnamed x32, local copies, waits for them, and re-layouts  8.01 us
    dot_general x3, matrix products, body(): lax.dot_general(stacks[time_tap], piece, (((1, 2, 3, 4), (1, 2, 3, 4)), (...  6.9 us
    all_to_all x1, waiting for transfers between devices, body(): lax.all_to_all(normed, 'ch', split_axis=2, concat_axis=0, tiled=True)  5.55 us
  transfers between devices with their start and end apart: 5, of which 4 were waited for; matrix products, arithmetic and copies ran while one was open for 6% of the time, Pallas kernels for 0%

commit v1 on v0

--- a/solution.py
+++ b/solution.py
@@ -166,7 +166,7 @@
         )
     grad_table = carry
     grad_table = grad_table.reshape(3, 3, 3, chans, full_width)
-    weight_grad = lax.psum(grad_table, ("ha", "dp"))
+    weight_grad = lax.psum(grad_table.astype(jnp.bfloat16), ("ha", "dp")).astype(jnp.float32)
     return (mixed, weight_grad)
 
 

time: 199 us -> 171 us (0.86)
  waiting for transfers between devices: 85 us -> 70.3 us
  blocking collectives: 51.1 us -> 37 us
  other arithmetic: 6.16 us -> 10.1 us
  local copies, waits for them, and re-layouts: 12.8 us -> 9.05 us
  starting transfers between devices: 11.4 us -> 14 us
    psum x1, waiting for transfers between devices: 77.4 us -> 54.7 us  [body(): lax.psum(grad_table.astype(jnp.bfloat16), ('ha', 'dp')).astype(jnp.float32)]
    all_to_all x1 -> x0, blocking collectives: 9.99 us -> none  [body(): lax.all_to_all(projected, 'ch', split_axis=0, concat_axis=2, tiled=True)]
    all_to_all x0 -> x1, waiting for transfers between devices: none -> 6.12 us  [body(): lax.all_to_all(projected, 'ch', split_axis=0, concat_axis=2, tiled=True)]
    all_gather x1, blocking collectives: 21.4 us -> 17.3 us  [body(): piece = lax.all_gather(masked_cot, 'ch', axis=0, tiled=True)]
    convert_element_type x0 -> x1, other arithmetic: none -> 3.98 us  [body(): lax.psum(grad_table.astype(jnp.bfloat16), ('ha', 'dp')).astype(jnp.float32)]
    unnamed x32 -> x41, local copies, waits for them, and re-layouts: 8.01 us -> 4.48 us
    all_to_all x0 -> x1, starting transfers between devices: none -> 3.5 us  [body(): lax.all_to_all(projected, 'ch', split_axis=0, concat_axis=2, tiled=True)]
    ppermute x1, waiting for transfers between devices: 0.43 us -> 3.87 us  [padded_2(): after = lax.ppermute(leading, axis, down)]
  transfers between devices with their start and end apart: 5 -> 6, of which waited for: 4 -> 4; matrix products, arithmetic and copies ran while one was open for 6% -> 7% of each run, Pallas kernels for 0% -> 0%
where the time goes in v1:
time: 171 us; the launch traced here: 170 us
  waiting for transfers between devices  70.3 us (41%)
  blocking collectives  37 us (22%)
  between operations  16.6 us (10%)
  starting transfers between devices  14 us (8%)
  matrix products  13.4 us (8%)
  other arithmetic  10.1 us (6%)
  local copies, waits for them, and re-layouts  9.05 us (5%)
    psum x1, waiting for transfers between devices, body(): lax.psum(grad_table.astype(jnp.bfloat16), ('ha', 'dp')).astype(jnp.float32)  54.7 us
    all_gather x1, blocking collectives, body(): piece = lax.all_gather(masked_cot, 'ch', axis=0, tiled=True)  17.3 us
    psum x2, blocking collectives, body(): first, second = lax.psum((first, second), 'ha')  10.8 us
    all_gather x1, blocking collectives, body(): piece = lax.all_gather(pairs, 'ha', axis=1, tiled=True)  8.94 us
    all_to_all x1, waiting for transfers between devices, body(): lax.all_to_all(projected, 'ch', split_axis=0, concat_axis=2, tiled=True)  6.12 us
    dot_general x3, matrix products, body(): lax.dot_general(part, stacks[time_tap], (((0,), (0,)), ((), ())), preferr...  5.78 us
    all_to_all x1, waiting for transfers between devices, body(): lax.all_to_all(normed, 'ch', split_axis=2, concat_axis=0, tiled=True)  5.55 us
    all_to_all x1, starting transfers between devices, body(): lax.all_to_all(normed, 'ch', split_axis=2, concat_axis=0, tiled=True)  5.54 us
  transfers between devices with their start and end apart: 6, of which 4 were waited for; matrix products, arithmetic and copies ran while one was open for 7% of the time, Pallas kernels for 0%

profile of v1, /device:TPU:0, one launch (start us, length us, event | category | flops | bytes accessed | tf_op | source)
XLA Modules:
  0.0 170.4 jit_solution(4983406673391585404)
XLA Ops:
  8.7 1.1 fusion.57
  10.4 5.9 %all-reduce.3 = (f32[8,1]{0,1:T(1,128)S(1)}, f32[8,1]{0,1:T(1,128)S(1)}) all-reduce(f32[8,1]{0,1:T(1,128)S(1)} %convolution_bitcast_fusion.3, f32[8,1]{0,1:T(1,128)S(1)} %convolution_bitcast_fusion.2), channel_id=1, replica_groups=mesh['ch'=4,'ha'=2,'dp'=4] {'ha'}, use_global_device_ids=true, to_apply=%region_2.0 | all-reduce | flops 16 | bytes 128 | tf_op jit(solution)/shard_map/psum | solution.py:98
  16.6 1.8 %fusion.78 = bf16[96,1,4,2,128]{4,0,3,1,2:T(8,128)(2,1)} fusion(f32[96]{0:T(128)} %param.16, f32[96]{0:T(128)} %param.15, f32[96]{0:T(128)S(1)} %mul.117, f32[96]{0:T(128)S(1)} %sub.66, bf16[96,1,4,2,128]{4,3,2,1,0:T(2,128)(2,1)} %param.13), kind=kLoop, calls=%fused_computation.84 | loop fusion | flops 589824 | bytes 394752 | tf_op jit(solution)/shard_map/convert_element_type | solution.py:99
  18.4 5.5 %all-to-all-start = ((bf16[96,1,4,2,128]{4,0,3,1,2:T(8,128)(2,1)}), bf16[96,1,4,2,128]{4,0,3,1,2:T(8,128)(2,1)S(1)}, u32[]{:S(2)}, u32[]{:S(2)}) async-start(bf16[96,1,4,2,128]{4,0,3,1,2:T(8,128)(2,1)} %fusion.78), calls=%async_computation | async-start | bytes 393216 | tf_op jit(solution)/shard_map/all_to_all | solution.py:102
  24.0 0.7 slice.120
  24.7 5.5 %all-to-all-done = bf16[96,1,4,2,128]{4,0,3,1,2:T(8,128)(2,1)S(1)} async-done(((bf16[96,1,4,2,128]{4,0,3,1,2:T(8,128)(2,1)}), bf16[96,1,4,2,128]{4,0,3,1,2:T(8,128)(2,1)S(1)}, u32[]{:S(2)}, u32[]{:S(2)}) %all-to-all-start) | async-done | bytes 196640 | tf_op jit(solution)/shard_map/all_to_all | solution.py:102
  30.4 1.5 fusion.37
  31.8 8.9 %all-gather = bf16[512,768]{1,0:T(8,128)(2,1)S(1)} all-gather(bf16[256,768]{1,0:T(8,128)(2,1)S(1)} %fusion.37), channel_id=2, replica_groups=mesh['ch'=4,'ha'=2,'dp'=4] {'ha'}, dimensions={0}, use_global_device_ids=true | all-gather | bytes 1179648 | tf_op jit(solution)/shard_map/all_gather | solution.py:121
  40.8 1.6 fusion.104
  42.7 0.6 fusion.46
  43.3 0.9 copy.33
  44.1 3.5 %all-to-all-start.1 = ((bf16[384,1,1,2,128]{4,3,2,1,0:T(2,128)(2,1)}), bf16[384,1,1,2,128]{4,3,2,1,0:T(2,128)(2,1)S(1)}, u32[]{:S(2)}, u32[]{:S(2)}) async-start(bf16[384,1,1,2,128]{4,3,2,1,0:T(2,128)(2,1)} %copy.33), calls=%async_computation.1 | async-start | bytes 393216 | tf_op jit(solution)/shard_map/all_to_all | solution.py:128
  47.8 6.1 %all-to-all-done.1 = bf16[384,1,1,2,128]{4,3,2,1,0:T(2,128)(2,1)S(1)} async-done(((bf16[384,1,1,2,128]{4,3,2,1,0:T(2,128)(2,1)}), bf16[384,1,1,2,128]{4,3,2,1,0:T(2,128)(2,1)S(1)}, u32[]{:S(2)}, u32[]{:S(2)}) %all-to-all-start.1) | async-done | bytes 196640 | tf_op jit(solution)/shard_map/all_to_all | solution.py:128
  54.8 17.3 %all_gather.7 = bf16[384,1,4,2,128]{4,0,3,2,1:T(8,128)(2,1)} all-gather(bf16[96,1,4,2,128]{4,0,3,2,1:T(8,128)(2,1)S(1)} %copy_multiply_fusion), channel_id=1, replica_groups=mesh['ch'=4,'ha'=2,'dp'=4] {'ch'}, dimensions={0}, use_global_device_ids=true | all-gather | bytes 983040 | tf_op jit(solution)/shard_map/all_gather | solution.py:155
  72.1 4.9 %all-reduce.2 = (f32[8,1]{0,1:T(1,128)S(1)}, f32[8,1]{0,1:T(1,128)S(1)}) all-reduce(f32[8,1]{0,1:T(1,128)S(1)} %convolution_bitcast_fusion.1, f32[8,1]{0,1:T(1,128)S(1)} %convolution_bitcast_fusion), channel_id=1, replica_groups=mesh['ch'=4,'ha'=2,'dp'=4] {'ha'}, use_global_device_ids=true, to_apply=%region_10.11 | all-reduce | flops 16 | bytes 128 | tf_op jit(solution)/shard_map/psum | solution.py:131
  77.7 3.4 %collective-permute-start = (bf16[96,1,4,1,128]{4,0,3,2,1:T(8,128)(2,1)S(1)}, bf16[96,1,4,1,128]{4,0,3,2,1:T(8,128)(2,1)S(1)}, u32[]{:S(2)}, u32[]{:S(2)}) collective-permute-start(bf16[96,1,4,1,128]{4,0,3,2,1:T(8,128)(2,1)S(1)} %get-tuple-element.47), channel_id=1, source_target_pairs={{0,4},{1,5},{2,6},{3,7},{8,12},{9,13},{10,14},{11,15},{16,20},{17,... | collective-permute-start | bytes 294920 | tf_op jit(solution)/shard_map/ppermute | solution.py:19
  81.1 1.3 collective-permute-start.1
  82.4 1.3 fusion.102
  83.7 3.9 %collective-permute-done.1 = bf16[96,1,4,1,128]{4,0,3,2,1:T(8,128)(2,1)S(1)} collective-permute-done((bf16[96,1,4,1,128]{4,0,3,2,1:T(8,128)(2,1)S(1)}, bf16[96,1,4,1,128]{4,0,3,2,1:T(8,128)(2,1)S(1)}, u32[]{:S(2)}, u32[]{:S(2)}) %collective-permute-start.1) | collective-permute-done | bytes 98336 | tf_op jit(solution)/shard_map/ppermute | solution.py:20
  87.6 0.4 fusion.41
  90.4 1.1 fusion.19
  92.1 1.2 fusion.25
  93.3 1.2 fusion.31
  94.5 1.3 copy-done.1
  96.1 2.8 %fusion.11 = f32[4,2,128,384]{2,3,1,0:T(8,128)S(1)} fusion(bf16[864,384,1,1]{1,0,3,2:T(8,128)(2,1)} %bitcast.175, bf16[864,1,4,2,128]{4,0,3,2,1:T(8,128)(2,1)} %copy-done.9), kind=kOutput, calls=%fused_computation.14 | convolution fusion | flops 679477248 | bytes 4005888 | tf_op jit(solution)/shard_map/dot_general | solution.py:142
  98.9 1.0 fusion.15
  100.0 0.4 copy-done.3
  100.4 2.0 %fusion.34 = bf16[384,1,4,2,128]{4,0,3,2,1:T(8,128)(2,1)} fusion(bf16[864,384,1,1]{1,0,3,2:T(8,128)(2,1)S(1)} %bitcast.169, bf16[864,1,4,2,128]{4,0,3,2,1:T(8,128)(2,1)S(1)} %copy-done.3, f32[4,2,128,384]{2,3,1,0:T(8,128)S(1)} %fusion.15, f32[4,2,128,384]{2,3,1,0:T(8,128)S(1)} %fusion.11), kind=kOutput, calls=%fused_computation.26 | convolution fusion | flops 680656896 | bytes 6365184 | tf_op jit(solution)/shard_map/dot_general | solution.py:142
  102.4 54.7 %all-reduce.6.cloned.1.call-done = bf16[3,3,3,96,384]{4,3,2,1,0:T(8,128)(2,1)} async-done(((bf16[3,3,3,96,384]{4,3,2,1,0:T(8,128)(2,1)}), bf16[3,3,3,96,384]{4,3,2,1,0:T(8,128)(2,1)}) %all-reduce.6.cloned.1.call-update) | async-done | bytes 1990672 | tf_op jit(solution)/shard_map/psum | solution.py:169
  157.1 4.0 %convert_element_type.145 = f32[3,3,3,96,384]{4,3,2,1,0:T(8,128)} convert(bf16[3,3,3,96,384]{4,3,2,1,0:T(8,128)(2,1)} %all-reduce.6.cloned.1.call-done) | non-fusion elementwise | flops 995328 | bytes 5971968 | tf_op jit(solution)/shard_map/convert_element_type | solution.py:169
  161.1 1.1 fusion.71
  162.1 0.8 copy.40
  (84 shorter events, 6.1 us)
Async XLA Ops:
  8.0 34.6 %copy-start = (bf16[384,384]{1,0:T(8,128)(2,1)S(1)}, bf16[384,384]{1,0:T(8,128)(2,1)}, u32[]{:S(2)}) copy-start(bf16[384,384]{1,0:T(8,128)(2,1)} %param.19) | copy-start | bytes 884740
  18.4 22.4 %slice-start = ((f32[1152]{0:T(1024)}), f32[384]{0:T(512)S(1)}, s32[]{:S(2)}) async-start(f32[1152]{0:T(1024)} %param.18), calls=%async_computation.5 | async-start | bytes 4096 | tf_op jit(solution)/shard_map/slice | solution.py:110
  18.4 11.8 %all-to-all-start = ((bf16[96,1,4,2,128]{4,0,3,1,2:T(8,128)(2,1)}), bf16[96,1,4,2,128]{4,0,3,1,2:T(8,128)(2,1)S(1)}, u32[]{:S(2)}, u32[]{:S(2)}) async-start(bf16[96,1,4,2,128]{4,0,3,1,2:T(8,128)(2,1)} %fusion.78), calls=%async_computation | async-start | bytes 393216 | tf_op jit(solution)/shard_map/all_to_all | solution.py:102
  31.8 10.8 %copy-start.15 = (f32[384]{0:T(512)S(1)}, f32[384]{0:T(512)}, u32[]{:S(2)}) copy-start(f32[384]{0:T(512)} %param.20) | copy-start | bytes 4612
  42.6 5.1 %copy-start.8 = (bf16[96,1,4,2,128]{4,3,2,1,0:T(2,128)(2,1)S(1)}, bf16[96,1,4,2,128]{4,3,2,1,0:T(2,128)(2,1)}, u32[]{:S(2)}) copy-start(bf16[96,1,4,2,128]{4,3,2,1,0:T(2,128)(2,1)} %param.25) | copy-start | bytes 589828
  42.6 11.3 %copy-start.5 = (bf16[96,1,4,2,128]{4,3,2,1,0:T(2,128)(2,1)S(1)}, bf16[96,1,4,2,128]{4,3,2,1,0:T(2,128)(2,1)}, u32[]{:S(2)}) copy-start(bf16[96,1,4,2,128]{4,3,2,1,0:T(2,128)(2,1)} %param.13) | copy-start | bytes 589828
  43.2 34.1 %copy-start.12 = (f32[96]{0:T(128)S(1)}, f32[96]{0:T(128)}, u32[]{:S(2)}) copy-start(f32[96]{0:T(128)} %param.22) | copy-start | bytes 1156
  43.3 34.1 %copy-start.13 = (f32[96]{0:T(128)S(1)}, f32[96]{0:T(128)}, u32[]{:S(2)}) copy-start(f32[96]{0:T(128)} %param.21) | copy-start | bytes 1156
  44.1 38.3 %copy-start.4 = (bf16[3,3,3,96,384]{4,3,2,1,0:T(8,128)(2,1)S(1)}, bf16[3,3,3,96,384]{4,3,2,1,0:T(8,128)(2,1)}, u32[]{:S(2)}) copy-start(bf16[3,3,3,96,384]{4,3,2,1,0:T(8,128)(2,1)} %param.23) | copy-start | bytes 5971972
  44.1 9.8 %all-to-all-start.1 = ((bf16[384,1,1,2,128]{4,3,2,1,0:T(2,128)(2,1)}), bf16[384,1,1,2,128]{4,3,2,1,0:T(2,128)(2,1)S(1)}, u32[]{:S(2)}, u32[]{:S(2)}) async-start(bf16[384,1,1,2,128]{4,3,2,1,0:T(2,128)(2,1)} %copy.33), calls=%async_computation.1 | async-start | bytes 393216 | tf_op jit(solution)/shard_map/all_to_all | solution.py:128
  47.6 109.4 %all-reduce.6.cloned.1.call-start = ((), (), s32[]{:S(2)}) async-start(), calls=%async_computation.4 | async-start | bytes 3981312 | tf_op jit(solution)/shard_map/psum | solution.py:169
  77.7 6.1 %collective-permute-start = (bf16[96,1,4,1,128]{4,0,3,2,1:T(8,128)(2,1)S(1)}, bf16[96,1,4,1,128]{4,0,3,2,1:T(8,128)(2,1)S(1)}, u32[]{:S(2)}, u32[]{:S(2)}) collective-permute-start(bf16[96,1,4,1,128]{4,0,3,2,1:T(8,128)(2,1)S(1)} %get-tuple-element.47), channel_id=1, source_target_pairs={{0,4},{1,5},{2,6},{3,7},{8,12},{9,13},{10,14},{11,15},{16,20},{17,... | collective-permute-start | bytes 294920 | tf_op jit(solution)/shard_map/ppermute | solution.py:19
  81.1 6.5 %collective-permute-start.1 = (bf16[96,1,4,1,128]{4,0,3,2,1:T(8,128)(2,1)S(1)}, bf16[96,1,4,1,128]{4,0,3,2,1:T(8,128)(2,1)S(1)}, u32[]{:S(2)}, u32[]{:S(2)}) collective-permute-start(bf16[96,1,4,1,128]{4,0,3,2,1:T(8,128)(2,1)S(1)} %get-tuple-element.48), channel_id=1, source_target_pairs={{4,0},{5,1},{6,2},{7,3},{12,8},{13,9},{14,10},{15,11},{20,16},{21,... | collective-permute-start | bytes 294920 | tf_op jit(solution)/shard_map/ppermute | solution.py:20
  89.2 1.1 copy-start.6
  90.3 1.2 copy-start.10
  90.3 1.8 %copy-start.9 = (bf16[864,1,4,2,128]{4,0,3,2,1:T(8,128)(2,1)}, bf16[864,1,4,2,128]{4,0,3,2,1:T(8,128)(2,1)S(1)}, u32[]{:S(2)}) copy-start(bf16[864,1,4,2,128]{4,0,3,2,1:T(8,128)(2,1)S(1)} %get-tuple-element.24) | copy-start | bytes 5308420
  91.9 1.4 copy-start.2
  94.5 1.3 copy-start.1
  95.8 65.2 %reduce-scatter.2.cloned.1.call-start = ((), (), s32[]{:S(2)}) async-start(), calls=%async_computation.3 | async-start | bytes 983040 | tf_op jit(solution)/shard_map/reduce_scatter | solution.py:145
  96.1 2.8 %copy-start.7 = (bf16[1,3,3,96,384]{4,3,2,1,0:T(8,128)(2,1)S(1)}, bf16[1,3,3,96,384]{4,3,2,1,0:T(8,128)(2,1)}, u32[]{:S(2)}) copy-start(bf16[1,3,3,96,384]{4,3,2,1,0:T(8,128)(2,1)} %get-tuple-element.22) | copy-start | bytes 1990660
  96.1 2.8 %copy-start.11 = (bf16[864,1,4,2,128]{4,0,3,2,1:T(8,128)(2,1)S(1)}, bf16[864,1,4,2,128]{4,0,3,2,1:T(8,128)(2,1)}, u32[]{:S(2)}) copy-start(bf16[864,1,4,2,128]{4,0,3,2,1:T(8,128)(2,1)} %copy-done.10) | copy-start | bytes 5308420
  98.9 1.5 copy-start.3
  102.4 58.7 %copy-start.14 = (f32[96]{0:T(128)S(1)}, f32[96]{0:T(128)}, u32[]{:S(2)}) copy-start(f32[96]{0:T(128)} %param.24) | copy-start | bytes 1156
Sparse Core Ops, SparseCore 0:
  96.0 61.0 all-reduce.5
Sparse Core Ops, SparseCore 1:
  102.5 22.9 reduce-scatter.1

commit v2 on v1

--- a/solution.py
+++ b/solution.py
@@ -73,6 +73,36 @@
                 ]
             )
     return jnp.concatenate(windows, axis=0)
+
+
+def butterfly_sum(table, axes):
+    steps = []
+    for axis in axes:
+        size = lax.axis_size(axis)
+        for bit in range(size.bit_length() - 1):
+            steps.append((axis, bit, size))
+    length = table.shape[0]
+    unit = (1 << len(steps)) * 8
+    padded = -(-length // unit) * unit
+    work = jnp.pad(table, ((0, padded - length), (0, 0)))
+    for axis, bit, size in steps:
+        side = (lax.axis_index(axis) >> bit) & 1
+        halves = work.reshape(2, work.shape[0] // 2, work.shape[1])
+        keep = lax.dynamic_index_in_dim(halves, side, keepdims=False)
+        send = lax.dynamic_index_in_dim(halves, 1 - side, keepdims=False)
+        perm = [(i, i ^ (1 << bit)) for i in range(size)]
+        got = lax.ppermute(send.astype(jnp.bfloat16), axis, perm)
+        work = keep + got.astype(jnp.float32)
+    work = work.astype(jnp.bfloat16)
+    for axis, bit, size in reversed(steps):
+        side = (lax.axis_index(axis) >> bit) & 1
+        perm = [(i, i ^ (1 << bit)) for i in range(size)]
+        got = lax.ppermute(work, axis, perm)
+        pair = jnp.stack([work, got])
+        first = lax.dynamic_index_in_dim(pair, side, keepdims=False)
+        second = lax.dynamic_index_in_dim(pair, 1 - side, keepdims=False)
+        work = jnp.concatenate([first, second], axis=0)
+    return work[:length].astype(jnp.float32)
 
 
 def body(
@@ -164,9 +194,8 @@
         carry = lax.dynamic_update_slice(
             carry, part[None], (jnp.int32(time_tap), jnp.int32(0), start)
         )
-    grad_table = carry
-    grad_table = grad_table.reshape(3, 3, 3, chans, full_width)
-    weight_grad = lax.psum(grad_table.astype(jnp.bfloat16), ("ha", "dp")).astype(jnp.float32)
+    weight_grad = butterfly_sum(carry.reshape(27 * chans, full_width), ("dp", "ha"))
+    weight_grad = weight_grad.reshape(3, 3, 3, chans, full_width)
     return (mixed, weight_grad)
 
 

time: 171 us -> 162 us (0.947)
  waiting for transfers between devices: 70.3 us -> 56.5 us
  starting transfers between devices: 14 us -> 18.5 us
  other arithmetic: 10.1 us -> 12.4 us
  matrix products: 13.4 us -> 11.4 us
  local copies, waits for them, and re-layouts: 9.05 us -> 11 us
    psum x1 -> x0, waiting for transfers between devices: 54.7 us -> none  [body(): lax.psum(grad_table.astype(jnp.bfloat16), ('ha', 'dp')).astype(jnp.float32)]
    ppermute x0 -> x6, waiting for transfers between devices: none -> 31.7 us  [the longest x3 19.1 us: butterfly_sum(): got = lax.ppermute(send.astype(jnp.bfloat16), axis, perm)]
    reduce_scatter x1, waiting for transfers between devices: 0.01 us -> 13.1 us  [body(): lax.psum_scatter(summed.astype(jnp.bfloat16), 'ch', scatter_dimension=0,...]
    convert_element_type x1, other arithmetic: 3.98 us -> 0.07 us  [butterfly_sum(): work = work.astype(jnp.bfloat16)]
    ppermute x1, waiting for transfers between devices: 3.87 us -> 0.01 us  [padded_2(): after = lax.ppermute(leading, axis, down)]
    ppermute x0 -> x6, starting transfers between devices: none -> 3.74 us  [the longest x3 2.01 us: butterfly_sum(): got = lax.ppermute(work, axis, perm)]
    reshape x0 -> x1, other arithmetic: none -> 2.42 us  [body(): weight_grad = weight_grad.reshape(3, 3, 3, chans, full_width)]
    add x0 -> x2, other arithmetic: none -> 1.82 us  [butterfly_sum(): work = keep + got.astype(jnp.float32)]
  transfers between devices with their start and end apart: 6 -> 11, of which waited for: 4 -> 8; matrix products, arithmetic and copies ran while one was open for 7% -> 5% of each run, Pallas kernels for 0% -> 0%
where the time goes in v2:
time: 162 us; the launch traced here: 161 us
  waiting for transfers between devices  56.5 us (35%)
  blocking collectives  36.5 us (23%)
  starting transfers between devices  18.5 us (11%)
  between operations  15.2 us (9%)
  other arithmetic  12.4 us (8%)
  matrix products  11.4 us (7%)
  local copies, waits for them, and re-layouts  11 us (7%)
    ppermute x3, waiting for transfers between devices, butterfly_sum(): got = lax.ppermute(send.astype(jnp.bfloat16), axis, perm)  19.1 us
    all_gather x1, blocking collectives, body(): piece = lax.all_gather(masked_cot, 'ch', axis=0, tiled=True)  16.8 us
    reduce_scatter x1, waiting for transfers between devices, body(): lax.psum_scatter(summed.astype(jnp.bfloat16), 'ch', scatter_dimension=0,...  13.1 us
    ppermute x3, waiting for transfers between devices, butterfly_sum(): got = lax.ppermute(work, axis, perm)  12.6 us
    psum x2, blocking collectives, body(): first, second = lax.psum((first, second), 'ha')  10.8 us
    all_gather x1, blocking collectives, body(): piece = lax.all_gather(pairs, 'ha', axis=1, tiled=True)  8.94 us
    all_to_all x1, waiting for transfers between devices, body(): lax.all_to_all(projected, 'ch', split_axis=0, concat_axis=2, tiled=True)  6.15 us
    all_to_all x1, waiting for transfers between devices, body(): lax.all_to_all(normed, 'ch', split_axis=2, concat_axis=0, tiled=True)  5.55 us
  transfers between devices with their start and end apart: 11, of which 8 were waited for; matrix products, arithmetic and copies ran while one was open for 5% of the time, Pallas kernels for 0%

profile of v2, /device:TPU:0, one launch (start us, length us, event | category | flops | bytes accessed | tf_op | source)
XLA Modules:
  0.0 161.5 jit_solution(3552810742932485537)
XLA Ops:
  7.2 1.2 fusion.68
  9.6 5.9 %all-reduce.4 = (f32[8,1]{0,1:T(1,128)S(1)}, f32[8,1]{0,1:T(1,128)S(1)}) all-reduce(f32[8,1]{0,1:T(1,128)S(1)} %convolution_bitcast_fusion.3, f32[8,1]{0,1:T(1,128)S(1)} %convolution_bitcast_fusion.2), channel_id=1, replica_groups=mesh['ch'=4,'ha'=2,'dp'=4] {'ha'}, use_global_device_ids=true, to_apply=%region_2.0 | all-reduce | flops 16 | bytes 128 | tf_op jit(solution)/shard_map/psum | solution.py:128
  15.8 1.8 %fusion.94 = bf16[96,1,4,2,128]{4,0,3,1,2:T(8,128)(2,1)} fusion(f32[96]{0:T(128)} %param.16, f32[96]{0:T(128)} %param.15, f32[96]{0:T(128)S(1)} %mul.117, f32[96]{0:T(128)S(1)} %sub.78, bf16[96,1,4,2,128]{4,3,2,1,0:T(2,128)(2,1)} %param.13), kind=kLoop, calls=%fused_computation.121 | loop fusion | flops 589824 | bytes 394752 | tf_op jit(solution)/shard_map/convert_element_type | solution.py:129
  17.6 5.5 %all-to-all-start = ((bf16[96,1,4,2,128]{4,0,3,1,2:T(8,128)(2,1)}), bf16[96,1,4,2,128]{4,0,3,1,2:T(8,128)(2,1)S(1)}, u32[]{:S(2)}, u32[]{:S(2)}) async-start(bf16[96,1,4,2,128]{4,0,3,1,2:T(8,128)(2,1)} %fusion.94), calls=%async_computation | async-start | bytes 393216 | tf_op jit(solution)/shard_map/all_to_all | solution.py:132
  23.8 5.5 %all-to-all-done = bf16[96,1,4,2,128]{4,0,3,1,2:T(8,128)(2,1)S(1)} async-done(((bf16[96,1,4,2,128]{4,0,3,1,2:T(8,128)(2,1)}), bf16[96,1,4,2,128]{4,0,3,1,2:T(8,128)(2,1)S(1)}, u32[]{:S(2)}, u32[]{:S(2)}) %all-to-all-start) | async-done | bytes 196640 | tf_op jit(solution)/shard_map/all_to_all | solution.py:132
  29.5 1.5 fusion.37
  31.0 8.9 %all-gather = bf16[512,768]{1,0:T(8,128)(2,1)S(1)} all-gather(bf16[256,768]{1,0:T(8,128)(2,1)S(1)} %fusion.37), channel_id=2, replica_groups=mesh['ch'=4,'ha'=2,'dp'=4] {'ha'}, dimensions={0}, use_global_device_ids=true | all-gather | bytes 1179648 | tf_op jit(solution)/shard_map/all_gather | solution.py:151
  40.0 1.6 fusion.122
  43.3 3.4 %all-to-all-start.1 = ((bf16[384,1,1,2,128]{4,3,2,1,0:T(2,128)(2,1)}), bf16[384,1,1,2,128]{4,3,2,1,0:T(2,128)(2,1)S(1)}, u32[]{:S(2)}, u32[]{:S(2)}) async-start(bf16[384,1,1,2,128]{4,3,2,1,0:T(2,128)(2,1)} %copy.33), calls=%async_computation.1 | async-start | bytes 393216 | tf_op jit(solution)/shard_map/all_to_all | solution.py:158
  46.7 6.2 %all-to-all-done.1 = bf16[384,1,1,2,128]{4,3,2,1,0:T(2,128)(2,1)S(1)} async-done(((bf16[384,1,1,2,128]{4,3,2,1,0:T(2,128)(2,1)}), bf16[384,1,1,2,128]{4,3,2,1,0:T(2,128)(2,1)S(1)}, u32[]{:S(2)}, u32[]{:S(2)}) %all-to-all-start.1) | async-done | bytes 196640 | tf_op jit(solution)/shard_map/all_to_all | solution.py:158
  53.8 5.0 %all-reduce.3 = (f32[8,1]{0,1:T(1,128)S(1)}, f32[8,1]{0,1:T(1,128)S(1)}) all-reduce(f32[8,1]{0,1:T(1,128)S(1)} %convolution_bitcast_fusion.1, f32[8,1]{0,1:T(1,128)S(1)} %convolution_bitcast_fusion), channel_id=1, replica_groups=mesh['ch'=4,'ha'=2,'dp'=4] {'ha'}, use_global_device_ids=true, to_apply=%region_10.11 | all-reduce | flops 16 | bytes 128 | tf_op jit(solution)/shard_map/psum | solution.py:161
  59.5 1.3 collective-permute-start.1
  60.8 4.6 %collective-permute-start = (bf16[96,1,4,1,128]{4,0,3,2,1:T(8,128)(2,1)S(1)}, bf16[96,1,4,1,128]{4,0,3,2,1:T(8,128)(2,1)S(1)}, u32[]{:S(2)}, u32[]{:S(2)}) collective-permute-start(bf16[96,1,4,1,128]{4,0,3,2,1:T(8,128)(2,1)S(1)} %get-tuple-element.57), channel_id=1, source_target_pairs={{0,4},{1,5},{2,6},{3,7},{8,12},{9,13},{10,14},{11,15},{16,20},{17,... | collective-permute-start | bytes 294920 | tf_op jit(solution)/shard_map/ppermute | solution.py:19
  65.4 16.8 %all_gather.7 = bf16[384,1,4,2,128]{4,0,3,2,1:T(8,128)(2,1)S(1)} all-gather(bf16[96,1,4,2,128]{4,0,3,2,1:T(8,128)(2,1)S(1)} %copy_multiply_fusion), channel_id=1, replica_groups=mesh['ch'=4,'ha'=2,'dp'=4] {'ch'}, dimensions={0}, use_global_device_ids=true | all-gather | bytes 983040 | tf_op jit(solution)/shard_map/all_gather | solution.py:185
  86.2 1.1 fusion.19
  87.6 1.1 fusion.25
  88.7 1.1 fusion.31
  90.1 1.9 %copy-done.1 = f32[2624,384]{1,0:T(8,128)} copy-done((f32[2624,384]{1,0:T(8,128)}, f32[2624,384]{1,0:T(8,128)S(1)}, u32[]{:S(2)}) %copy-start.1) | copy-done | bytes 4030488
  92.1 2.6 %collective-permute-done.2 = bf16[1312,384]{1,0:T(8,128)(2,1)S(1)} collective-permute-done((bf16[1312,384]{1,0:T(8,128)(2,1)S(1)}, bf16[1312,384]{1,0:T(8,128)(2,1)S(1)}, u32[]{:S(2)}, u32[]{:S(2)}) %collective-permute-start.2) | collective-permute-done | bytes 1007648 | tf_op jit(solution)/shard_map/ppermute | solution.py:94
  94.7 1.7 %bitcast_add_fusion = f32[1312,384]{1,0:T(8,128)S(1)} fusion(bf16[1312,384]{1,0:T(8,128)(2,1)S(1)} %collective-permute-done.2, f32[2,1312,384]{2,1,0:T(8,128)} %bitcast.209, s32[]{:T(128)S(6)} %select_n.30), kind=kLoop, calls=%fused_computation.12 | loop fusion | flops 1007616 | bytes 5038084 | tf_op jit(solution)/shard_map/add | solution.py:95
  96.5 1.6 collective-permute-start.3
  98.1 1.7 %fusion.120 = (bf16[1,3,3,96,384]{4,3,2,1,0:T(8,128)(2,1)S(1)}, bf16[1,3,3,96,384]{4,3,2,1,0:T(8,128)(2,1)S(1)}, bf16[1,3,3,96,384]{4,3,2,1,0:T(8,128)(2,1)S(1)}) fusion(bf16[3,3,3,96,384]{4,3,2,1,0:T(8,128)(2,1)} %param.23), kind=kLoop, calls=%fused_computation.180 | loop fusion | bytes 3981312 | tf_op jit(solution)/shard_map/slice | solution.py:171
  99.8 10.3 %collective-permute-done.3 = bf16[656,384]{1,0:T(8,128)(2,1)S(1)} collective-permute-done((bf16[656,384]{1,0:T(8,128)(2,1)S(1)}, bf16[656,384]{1,0:T(8,128)(2,1)S(1)}, u32[]{:S(2)}, u32[]{:S(2)}) %collective-permute-start.3) | collective-permute-done | bytes 503840 | tf_op jit(solution)/shard_map/ppermute | solution.py:94
  111.4 6.2 %collective-permute-done.4 = bf16[328,384]{1,0:T(8,128)(2,1)S(1)} collective-permute-done((bf16[328,384]{1,0:T(8,128)(2,1)S(1)}, bf16[328,384]{1,0:T(8,128)(2,1)S(1)}, u32[]{:S(2)}, u32[]{:S(2)}) %collective-permute-start.4) | collective-permute-done | bytes 251936 | tf_op jit(solution)/shard_map/ppermute | solution.py:94
  118.0 1.0 fusion.11
  119.1 5.1 %collective-permute-done.5 = bf16[328,384]{1,0:T(8,128)(2,1)S(1)} collective-permute-done((bf16[328,384]{1,0:T(8,128)(2,1)S(1)}, bf16[328,384]{1,0:T(8,128)(2,1)S(1)}, u32[]{:S(2)}, u32[]{:S(2)}) %collective-permute-start.5) | collective-permute-done | bytes 251936 | tf_op jit(solution)/shard_map/ppermute | solution.py:100
  124.5 1.6 collective-permute-start.6
  126.0 1.9 %fusion.34 = bf16[384,1,4,2,128]{4,0,3,2,1:T(8,128)(2,1)} fusion(bf16[864,384,1,1]{1,0,3,2:T(8,128)(2,1)S(1)} %bitcast.215, bf16[864,1,4,2,128]{4,0,3,2,1:T(8,128)(2,1)S(1)} %copy-done.3, f32[4,2,128,384]{2,3,1,0:T(8,128)S(1)} %fusion.15, f32[4,2,128,384]{2,3,1,0:T(8,128)S(1)} %fusion.11), kind=kOutput, calls=%fused_computation.33 | convolution fusion | flops 680656896 | bytes 6365184 | tf_op jit(solution)/shard_map/dot_general | solution.py:172
  128.0 7.5 %collective-permute-done.6 = bf16[656,384]{1,0:T(8,128)(2,1)S(1)} collective-permute-done((bf16[656,384]{1,0:T(8,128)(2,1)S(1)}, bf16[656,384]{1,0:T(8,128)(2,1)S(1)}, u32[]{:S(2)}, u32[]{:S(2)}) %collective-permute-start.6) | collective-permute-done | bytes 503840 | tf_op jit(solution)/shard_map/ppermute | solution.py:100
  136.2 13.1 %reduce-scatter.2.cloned.1.call-done = bf16[96,1,4,2,128]{4,0,3,2,1:T(8,128)(2,1)} async-done(((bf16[384,1,4,2,128]{4,0,3,2,1:T(8,128)(2,1)}), bf16[96,1,4,2,128]{4,0,3,2,1:T(8,128)(2,1)}) %reduce-scatter.2.cloned.1.call-update) | async-done | bytes 196624 | tf_op jit(solution)/shard_map/reduce_scatter | solution.py:175
  149.3 1.1 fusion.82
  152.2 2.4 %convert.5 = f32[3,3,3,96,384]{4,3,2,1,0:T(8,128)} convert(bf16[3,3,3,96,384]{4,3,2,1,0:T(8,128)(2,1)S(1)} %bitcast.210) | non-fusion elementwise | flops 995328 | bytes 5971968 | tf_op jit(solution)/shard_map/reshape | solution.py:198
  (102 shorter events, 14.3 us)
Async XLA Ops:
  7.2 34.6 %copy-start = (bf16[384,384]{1,0:T(8,128)(2,1)S(1)}, bf16[384,384]{1,0:T(8,128)(2,1)}, u32[]{:S(2)}) copy-start(bf16[384,384]{1,0:T(8,128)(2,1)} %param.19) | copy-start | bytes 884740
  17.6 22.4 %slice-start = ((f32[1152]{0:T(1024)}), f32[384]{0:T(512)S(1)}, s32[]{:S(2)}) async-start(f32[1152]{0:T(1024)} %param.18), calls=%async_computation.4 | async-start | bytes 4096 | tf_op jit(solution)/shard_map/slice | solution.py:140
  17.6 11.8 %all-to-all-start = ((bf16[96,1,4,2,128]{4,0,3,1,2:T(8,128)(2,1)}), bf16[96,1,4,2,128]{4,0,3,1,2:T(8,128)(2,1)S(1)}, u32[]{:S(2)}, u32[]{:S(2)}) async-start(bf16[96,1,4,2,128]{4,0,3,1,2:T(8,128)(2,1)} %fusion.94), calls=%async_computation | async-start | bytes 393216 | tf_op jit(solution)/shard_map/all_to_all | solution.py:132
  31.0 10.8 %copy-start.13 = (f32[384]{0:T(512)S(1)}, f32[384]{0:T(512)}, u32[]{:S(2)}) copy-start(f32[384]{0:T(512)} %param.20) | copy-start | bytes 4612
  41.8 11.1 %copy-start.4 = (bf16[96,1,4,2,128]{4,3,2,1,0:T(2,128)(2,1)S(1)}, bf16[96,1,4,2,128]{4,3,2,1,0:T(2,128)(2,1)}, u32[]{:S(2)}) copy-start(bf16[96,1,4,2,128]{4,3,2,1,0:T(2,128)(2,1)} %param.13) | copy-start | bytes 589828
  41.8 11.9 %copy-start.5 = (bf16[96,1,4,2,128]{4,3,2,1,0:T(2,128)(2,1)S(1)}, bf16[96,1,4,2,128]{4,3,2,1,0:T(2,128)(2,1)}, u32[]{:S(2)}) copy-start(bf16[96,1,4,2,128]{4,3,2,1,0:T(2,128)(2,1)} %param.25) | copy-start | bytes 589828
  42.4 16.7 %copy-start.10 = (f32[96]{0:T(128)S(1)}, f32[96]{0:T(128)}, u32[]{:S(2)}) copy-start(f32[96]{0:T(128)} %param.22) | copy-start | bytes 1156
  42.4 16.7 %copy-start.11 = (f32[96]{0:T(128)S(1)}, f32[96]{0:T(128)}, u32[]{:S(2)}) copy-start(f32[96]{0:T(128)} %param.21) | copy-start | bytes 1156
  43.3 9.6 %all-to-all-start.1 = ((bf16[384,1,1,2,128]{4,3,2,1,0:T(2,128)(2,1)}), bf16[384,1,1,2,128]{4,3,2,1,0:T(2,128)(2,1)S(1)}, u32[]{:S(2)}, u32[]{:S(2)}) async-start(bf16[384,1,1,2,128]{4,3,2,1,0:T(2,128)(2,1)} %copy.33), calls=%async_computation.1 | async-start | bytes 393216 | tf_op jit(solution)/shard_map/all_to_all | solution.py:158
  46.7 102.6 %reduce-scatter.2.cloned.1.call-start = ((), (), s32[]{:S(2)}) async-start(), calls=%async_computation.3 | async-start | bytes 983040 | tf_op jit(solution)/shard_map/reduce_scatter | solution.py:175
  59.5 22.6 %collective-permute-start.1 = (bf16[96,1,4,1,128]{4,0,3,2,1:T(8,128)(2,1)S(1)}, bf16[96,1,4,1,128]{4,0,3,2,1:T(8,128)(2,1)S(1)}, u32[]{:S(2)}, u32[]{:S(2)}) collective-permute-start(bf16[96,1,4,1,128]{4,0,3,2,1:T(8,128)(2,1)S(1)} %get-tuple-element.58), channel_id=1, source_target_pairs={{4,0},{5,1},{6,2},{7,3},{12,8},{13,9},{14,10},{15,11},{20,16},{21,... | collective-permute-start | bytes 294920 | tf_op jit(solution)/shard_map/ppermute | solution.py:20
  60.8 21.3 %collective-permute-start = (bf16[96,1,4,1,128]{4,0,3,2,1:T(8,128)(2,1)S(1)}, bf16[96,1,4,1,128]{4,0,3,2,1:T(8,128)(2,1)S(1)}, u32[]{:S(2)}, u32[]{:S(2)}) collective-permute-start(bf16[96,1,4,1,128]{4,0,3,2,1:T(8,128)(2,1)S(1)} %get-tuple-element.57), channel_id=1, source_target_pairs={{0,4},{1,5},{2,6},{3,7},{8,12},{9,13},{10,14},{11,15},{16,20},{17,... | collective-permute-start | bytes 294920 | tf_op jit(solution)/shard_map/ppermute | solution.py:19
  84.9 1.2 copy-start.8
  84.9 2.6 %copy-start.6 = (bf16[864,1,4,2,128]{4,0,3,2,1:T(8,128)(2,1)}, bf16[864,1,4,2,128]{4,0,3,2,1:T(8,128)(2,1)S(1)}, u32[]{:S(2)}) copy-start(bf16[864,1,4,2,128]{4,0,3,2,1:T(8,128)(2,1)S(1)} %get-tuple-element.26) | copy-start | bytes 5308420
  85.1 3.5 %copy-start.2 = (bf16[864,1,4,2,128]{4,0,3,2,1:T(8,128)(2,1)}, bf16[864,1,4,2,128]{4,0,3,2,1:T(8,128)(2,1)S(1)}, u32[]{:S(2)}) copy-start(bf16[864,1,4,2,128]{4,0,3,2,1:T(8,128)(2,1)S(1)} %slice_dynamic-update-slice_fusion) | copy-start | bytes 5308420
  90.0 1.9 %copy-start.1 = (f32[2624,384]{1,0:T(8,128)}, f32[2624,384]{1,0:T(8,128)S(1)}, u32[]{:S(2)}) copy-start(f32[2624,384]{1,0:T(8,128)S(1)} %pad.10) | copy-start | bytes 12091396
  92.1 2.7 %collective-permute-start.2 = (bf16[1312,384]{1,0:T(8,128)(2,1)S(1)}, bf16[1312,384]{1,0:T(8,128)(2,1)S(1)}, u32[]{:S(2)}, u32[]{:S(2)}) collective-permute-start(bf16[1312,384]{1,0:T(8,128)(2,1)S(1)} %fusion.47), channel_id=1, source_target_pairs={{0,1},{1,0},{2,3},{3,2},{4,5},{5,4},{6,7},{7,6},{8,9},{9,8},{10,11... | collective-permute-start | bytes 3022856 | tf_op jit(solution)/shard_map/ppermute | solution.py:94
  96.5 13.6 %collective-permute-start.3 = (bf16[656,384]{1,0:T(8,128)(2,1)S(1)}, bf16[656,384]{1,0:T(8,128)(2,1)S(1)}, u32[]{:S(2)}, u32[]{:S(2)}) collective-permute-start(bf16[656,384]{1,0:T(8,128)(2,1)S(1)} %fusion.56), channel_id=1, source_target_pairs={{0,2},{1,3},{2,0},{3,1},{4,6},{5,7},{6,4},{7,5},{8,10},{9,11},{10,... | collective-permute-start | bytes 1511432 | tf_op jit(solution)/shard_map/ppermute | solution.py:94
  99.8 10.5 %copy-start.9 = (bf16[864,1,4,2,128]{4,0,3,2,1:T(8,128)(2,1)S(1)}, bf16[864,1,4,2,128]{4,0,3,2,1:T(8,128)(2,1)}, u32[]{:S(2)}) copy-start(bf16[864,1,4,2,128]{4,0,3,2,1:T(8,128)(2,1)} %copy-done.8) | copy-start | bytes 5308420
  110.3 7.3 %collective-permute-start.4 = (bf16[328,384]{1,0:T(8,128)(2,1)S(1)}, bf16[328,384]{1,0:T(8,128)(2,1)S(1)}, u32[]{:S(2)}, u32[]{:S(2)}) collective-permute-start(bf16[328,384]{1,0:T(8,128)(2,1)S(1)} %fusion.89), channel_id=1, source_target_pairs={{0,4},{4,0},{1,5},{5,1},{2,6},{6,2},{3,7},{7,3},{8,12},{12,8},{9,1... | collective-permute-start | bytes 755720 | tf_op jit(solution)/shard_map/ppermute | solution.py:94
  110.3 7.7 %copy-start.7 = (bf16[864,1,4,2,128]{4,0,3,2,1:T(8,128)(2,1)S(1)}, bf16[864,1,4,2,128]{4,0,3,2,1:T(8,128)(2,1)}, u32[]{:S(2)}) copy-start(bf16[864,1,4,2,128]{4,0,3,2,1:T(8,128)(2,1)} %copy-done.6) | copy-start | bytes 5308420
  117.7 6.5 %collective-permute-start.5 = (bf16[328,384]{1,0:T(8,128)(2,1)S(1)}, bf16[328,384]{1,0:T(8,128)(2,1)S(1)}, u32[]{:S(2)}, u32[]{:S(2)}) collective-permute-start(bf16[328,384]{1,0:T(8,128)(2,1)S(1)} %fusion.61), channel_id=1, source_target_pairs={{0,4},{4,0},{1,5},{5,1},{2,6},{6,2},{3,7},{7,3},{8,12},{12,8},{9,1... | collective-permute-start | bytes 755720 | tf_op jit(solution)/shard_map/ppermute | solution.py:100
  119.1 7.0 %copy-start.3 = (bf16[864,1,4,2,128]{4,0,3,2,1:T(8,128)(2,1)S(1)}, bf16[864,1,4,2,128]{4,0,3,2,1:T(8,128)(2,1)}, u32[]{:S(2)}) copy-start(bf16[864,1,4,2,128]{4,0,3,2,1:T(8,128)(2,1)} %copy-done.2) | copy-start | bytes 5308420
  124.5 11.0 %collective-permute-start.6 = (bf16[656,384]{1,0:T(8,128)(2,1)S(1)}, bf16[656,384]{1,0:T(8,128)(2,1)S(1)}, u32[]{:S(2)}, u32[]{:S(2)}) collective-permute-start(bf16[656,384]{1,0:T(8,128)(2,1)S(1)} %get-tuple-element.53), channel_id=1, source_target_pairs={{0,2},{1,3},{2,0},{3,1},{4,6},{5,7},{6,4},{7,5},{8,10},{9,11},{10,... | collective-permute-start | bytes 1511432 | tf_op jit(solution)/shard_map/ppermute | solution.py:100
  135.9 13.4 %copy-start.12 = (f32[96]{0:T(128)S(1)}, f32[96]{0:T(128)}, u32[]{:S(2)}) copy-start(f32[96]{0:T(128)} %param.24) | copy-start | bytes 1156
  136.1 15.1 %collective-permute-start.7 = (bf16[1312,384]{1,0:T(8,128)(2,1)S(1)}, bf16[1312,384]{1,0:T(8,128)(2,1)S(1)}, u32[]{:S(2)}, u32[]{:S(2)}) collective-permute-start(bf16[1312,384]{1,0:T(8,128)(2,1)S(1)} %get-tuple-element.49), channel_id=1, source_target_pairs={{0,1},{1,0},{2,3},{3,2},{4,5},{5,4},{6,7},{7,6},{8,9},{9,8},{10,11... | collective-permute-start | bytes 3022856 | tf_op jit(solution)/shard_map/ppermute | solution.py:100
Sparse Core Ops, SparseCore 0:
  128.1 21.1 reduce-scatter.1

commit v3 on v2

--- a/solution.py
+++ b/solution.py
@@ -172,9 +172,11 @@
         summed = summed + lax.dot_general(
             part, stacks[time_tap], (((0,), (0,)), ((), ())), preferred_element_type=jnp.float32
         )
-    conv_out = lax.psum_scatter(
-        summed.astype(jnp.bfloat16), "ch", scatter_dimension=0, tiled=True
-    ).astype(jnp.float32)
+    summed, stacks = lax.optimization_barrier((summed.astype(jnp.bfloat16), stacks))
+    shares = lax.axis_size("ch")
+    parts = summed.reshape((shares, amount // shares) + summed.shape[1:])
+    parts = lax.all_to_all(parts, "ch", split_axis=0, concat_axis=0, tiled=True)
+    conv_out = jnp.sum(parts.astype(jnp.float32), axis=0)
     mixed = mask[None, :, :, None, None] * (
         hidden.astype(jnp.float32) + conv_out + conv_bias[:, None, None, None, None]
     )

time: 162 us -> 160 us (0.988)
  between operations: 15.2 us -> 1.8 us
  other arithmetic: 12.4 us -> 15.6 us
  starting transfers between devices: 18.5 us -> 21.6 us
  waiting for transfers between devices: 56.5 us -> 59.5 us
  local copies, waits for them, and re-layouts: 11 us -> 12.9 us
    reduce_scatter x1 -> x0, waiting for transfers between devices: 13.1 us -> none  [body(): lax.psum_scatter(summed.astype(jnp.bfloat16), 'ch', scatter_dimension=0,...]
    all_to_all x0 -> x1, waiting for transfers between devices: none -> 11.9 us  [body(): parts = lax.all_to_all(parts, 'ch', split_axis=0, concat_axis=0, tiled=True)]
    all_to_all x0 -> x1, starting transfers between devices: none -> 4.18 us  [body(): parts = lax.all_to_all(parts, 'ch', split_axis=0, concat_axis=0, tiled=True)]
    ppermute x1, waiting for transfers between devices: 0.01 us -> 3.3 us  [padded_2(): after = lax.ppermute(leading, axis, down)]
    ppermute x3, waiting for transfers between devices: 19.1 us -> 22.3 us  [butterfly_sum(): got = lax.ppermute(send.astype(jnp.bfloat16), axis, perm)]
    ppermute x3, waiting for transfers between devices: 12.6 us -> 10.2 us  [butterfly_sum(): got = lax.ppermute(work, axis, perm)]
    concatenate x3, other arithmetic: 0.47 us -> 2.2 us  [butterfly_sum(): work = jnp.concatenate([first, second], axis=0)]
    unnamed x37 -> x29, local copies, waits for them, and re-layouts: 5.46 us -> 5.27 us
  transfers between devices with their start and end apart: 11 -> 11, of which waited for: 8 -> 9; matrix products, arithmetic and copies ran while one was open for 5% -> 4% of each run, Pallas kernels for 0% -> 0%
where the time goes in v3:
time: 160 us
  waiting for transfers between devices  59.5 us (37%)
  blocking collectives  37 us (23%)
  starting transfers between devices  21.6 us (14%)
  other arithmetic  15.6 us (10%)
  local copies, waits for them, and re-layouts  12.9 us (8%)
  matrix products  11.1 us (7%)
  between operations  1.8 us (1%)
    ppermute x3, waiting for transfers between devices, butterfly_sum(): got = lax.ppermute(send.astype(jnp.bfloat16), axis, perm)  22.3 us
    all_gather x1, blocking collectives, body(): piece = lax.all_gather(masked_cot, 'ch', axis=0, tiled=True)  17.3 us
    all_to_all x1, waiting for transfers between devices, body(): parts = lax.all_to_all(parts, 'ch', split_axis=0, concat_axis=0, tiled=True)  11.9 us
    psum x2, blocking collectives, body(): first, second = lax.psum((first, second), 'ha')  10.8 us
    ppermute x3, waiting for transfers between devices, butterfly_sum(): got = lax.ppermute(work, axis, perm)  10.2 us
    all_gather x1, blocking collectives, body(): piece = lax.all_gather(pairs, 'ha', axis=1, tiled=True)  8.94 us
    all_to_all x1, waiting for transfers between devices, body(): lax.all_to_all(projected, 'ch', split_axis=0, concat_axis=2, tiled=True)  6.17 us
    all_to_all x1, waiting for transfers between devices, body(): lax.all_to_all(normed, 'ch', split_axis=2, concat_axis=0, tiled=True)  5.55 us
  transfers between devices with their start and end apart: 11, of which 9 were waited for; matrix products, arithmetic and copies ran while one was open for 4% of the time, Pallas kernels for 0%

profile of v3, /device:TPU:0, one launch (start us, length us, event | category | flops | bytes accessed | tf_op | source)
XLA Modules:
  0.0 159.6 jit_solution(362209770929733705)
XLA Ops:
  1.3 1.1 fusion.68
  3.1 5.9 %all-reduce.4 = (f32[8,1]{0,1:T(1,128)S(1)}, f32[8,1]{0,1:T(1,128)S(1)}) all-reduce(f32[8,1]{0,1:T(1,128)S(1)} %convolution_bitcast_fusion.3, f32[8,1]{0,1:T(1,128)S(1)} %convolution_bitcast_fusion.2), channel_id=1, replica_groups=mesh['ch'=4,'ha'=2,'dp'=4] {'ha'}, use_global_device_ids=true, to_apply=%region_2.0 | all-reduce | flops 16 | bytes 128 | tf_op jit(solution)/shard_map/psum | solution.py:128
  9.2 1.8 %fusion.94 = bf16[96,1,4,2,128]{4,0,3,1,2:T(8,128)(2,1)} fusion(f32[96]{0:T(128)} %param.16, f32[96]{0:T(128)} %param.15, f32[96]{0:T(128)S(1)} %mul.117, f32[96]{0:T(128)S(1)} %sub.78, bf16[96,1,4,2,128]{4,3,2,1,0:T(2,128)(2,1)} %param.13), kind=kLoop, calls=%fused_computation.122 | loop fusion | flops 589824 | bytes 394752 | tf_op jit(solution)/shard_map/convert_element_type | solution.py:129
  11.1 5.5 %all-to-all-start = ((bf16[96,1,4,2,128]{4,0,3,1,2:T(8,128)(2,1)}), bf16[96,1,4,2,128]{4,0,3,1,2:T(8,128)(2,1)S(1)}, u32[]{:S(2)}, u32[]{:S(2)}) async-start(bf16[96,1,4,2,128]{4,0,3,1,2:T(8,128)(2,1)} %fusion.94), calls=%async_computation | async-start | bytes 393216 | tf_op jit(solution)/shard_map/all_to_all | solution.py:132
  17.3 5.5 %all-to-all-done = bf16[96,1,4,2,128]{4,0,3,1,2:T(8,128)(2,1)S(1)} async-done(((bf16[96,1,4,2,128]{4,0,3,1,2:T(8,128)(2,1)}), bf16[96,1,4,2,128]{4,0,3,1,2:T(8,128)(2,1)S(1)}, u32[]{:S(2)}, u32[]{:S(2)}) %all-to-all-start) | async-done | bytes 196640 | tf_op jit(solution)/shard_map/all_to_all | solution.py:132
  23.0 1.5 fusion.37
  24.5 8.9 %all-gather = bf16[512,768]{1,0:T(8,128)(2,1)S(1)} all-gather(bf16[256,768]{1,0:T(8,128)(2,1)S(1)} %fusion.37), channel_id=2, replica_groups=mesh['ch'=4,'ha'=2,'dp'=4] {'ha'}, dimensions={0}, use_global_device_ids=true | all-gather | bytes 1179648 | tf_op jit(solution)/shard_map/all_gather | solution.py:151
  33.4 1.6 fusion.122
  36.7 3.4 %all-to-all-start.1 = ((bf16[384,1,1,2,128]{4,3,2,1,0:T(2,128)(2,1)}), bf16[384,1,1,2,128]{4,3,2,1,0:T(2,128)(2,1)S(1)}, u32[]{:S(2)}, u32[]{:S(2)}) async-start(bf16[384,1,1,2,128]{4,3,2,1,0:T(2,128)(2,1)} %copy.28), calls=%async_computation.1 | async-start | bytes 393216 | tf_op jit(solution)/shard_map/all_to_all | solution.py:158
  40.2 6.2 %all-to-all-done.1 = bf16[384,1,1,2,128]{4,3,2,1,0:T(2,128)(2,1)S(1)} async-done(((bf16[384,1,1,2,128]{4,3,2,1,0:T(2,128)(2,1)}), bf16[384,1,1,2,128]{4,3,2,1,0:T(2,128)(2,1)S(1)}, u32[]{:S(2)}, u32[]{:S(2)}) %all-to-all-start.1) | async-done | bytes 196640 | tf_op jit(solution)/shard_map/all_to_all | solution.py:158
  47.3 17.3 %all_gather.7 = bf16[384,1,4,2,128]{4,0,3,2,1:T(8,128)(2,1)} all-gather(bf16[96,1,4,2,128]{4,0,3,2,1:T(8,128)(2,1)S(1)} %copy_multiply_fusion), channel_id=1, replica_groups=mesh['ch'=4,'ha'=2,'dp'=4] {'ch'}, dimensions={0}, use_global_device_ids=true | all-gather | bytes 983040 | tf_op jit(solution)/shard_map/all_gather | solution.py:187
  64.6 4.9 %all-reduce.3 = (f32[8,1]{0,1:T(1,128)S(1)}, f32[8,1]{0,1:T(1,128)S(1)}) all-reduce(f32[8,1]{0,1:T(1,128)S(1)} %convolution_bitcast_fusion.1, f32[8,1]{0,1:T(1,128)S(1)} %convolution_bitcast_fusion), channel_id=1, replica_groups=mesh['ch'=4,'ha'=2,'dp'=4] {'ha'}, use_global_device_ids=true, to_apply=%region_10.11 | all-reduce | flops 16 | bytes 128 | tf_op jit(solution)/shard_map/psum | solution.py:161
  70.2 3.5 %collective-permute-start = (bf16[96,1,4,1,128]{4,0,3,2,1:T(8,128)(2,1)S(1)}, bf16[96,1,4,1,128]{4,0,3,2,1:T(8,128)(2,1)S(1)}, u32[]{:S(2)}, u32[]{:S(2)}) collective-permute-start(bf16[96,1,4,1,128]{4,0,3,2,1:T(8,128)(2,1)S(1)} %get-tuple-element.65), channel_id=1, source_target_pairs={{0,4},{1,5},{2,6},{3,7},{8,12},{9,13},{10,14},{11,15},{16,20},{17,... | collective-permute-start | bytes 294920 | tf_op jit(solution)/shard_map/ppermute | solution.py:19
  73.7 1.5 collective-permute-start.1
  75.2 1.7 %fusion.120 = (bf16[1,3,3,96,384]{4,3,2,1,0:T(8,128)(2,1)S(1)}, bf16[1,3,3,96,384]{4,3,2,1,0:T(8,128)(2,1)S(1)}, bf16[1,3,3,96,384]{4,3,2,1,0:T(8,128)(2,1)S(1)}) fusion(bf16[3,3,3,96,384]{4,3,2,1,0:T(8,128)(2,1)} %param.23), kind=kLoop, calls=%fused_computation.181 | loop fusion | bytes 3981312 | tf_op jit(solution)/shard_map/slice | solution.py:171
  76.9 3.3 %collective-permute-done.1 = bf16[96,1,4,1,128]{4,0,3,2,1:T(8,128)(2,1)S(1)} collective-permute-done((bf16[96,1,4,1,128]{4,0,3,2,1:T(8,128)(2,1)S(1)}, bf16[96,1,4,1,128]{4,0,3,2,1:T(8,128)(2,1)S(1)}, u32[]{:S(2)}, u32[]{:S(2)}) %collective-permute-start.1) | collective-permute-done | bytes 98336 | tf_op jit(solution)/shard_map/ppermute | solution.py:20
  83.1 1.2 fusion.13
  84.3 1.2 fusion.15
  85.6 1.3 fusion.34
  90.7 1.9 %copy-done.1 = f32[2624,384]{1,0:T(8,128)} copy-done((f32[2624,384]{1,0:T(8,128)}, f32[2624,384]{1,0:T(8,128)S(1)}, u32[]{:S(2)}) %copy-start.1) | copy-done | bytes 4030488
  92.8 2.7 %collective-permute-done.2 = bf16[1312,384]{1,0:T(8,128)(2,1)} collective-permute-done((bf16[1312,384]{1,0:T(8,128)(2,1)S(1)}, bf16[1312,384]{1,0:T(8,128)(2,1)}, u32[]{:S(2)}, u32[]{:S(2)}) %collective-permute-start.2) | collective-permute-done | bytes 1007648 | tf_op jit(solution)/shard_map/ppermute | solution.py:94
  95.5 2.0 %bitcast_add_fusion = f32[1312,384]{1,0:T(8,128)S(1)} fusion(bf16[1312,384]{1,0:T(8,128)(2,1)} %collective-permute-done.2, f32[2,1312,384]{2,1,0:T(8,128)} %bitcast.215, s32[]{:T(128)S(6)} %select_n.30), kind=kLoop, calls=%fused_computation.12 | loop fusion | flops 1007616 | bytes 5038084 | tf_op jit(solution)/shard_map/add | solution.py:95
  98.4 1.5 collective-permute-start.3
  99.9 12.3 %collective-permute-done.3 = bf16[656,384]{1,0:T(8,128)(2,1)} collective-permute-done((bf16[656,384]{1,0:T(8,128)(2,1)}, bf16[656,384]{1,0:T(8,128)(2,1)}, u32[]{:S(2)}, u32[]{:S(2)}) %collective-permute-start.3) | collective-permute-done | bytes 503840 | tf_op jit(solution)/shard_map/ppermute | solution.py:94
  114.4 7.3 %collective-permute-done.4 = bf16[328,384]{1,0:T(8,128)(2,1)S(1)} collective-permute-done((bf16[328,384]{1,0:T(8,128)(2,1)S(1)}, bf16[328,384]{1,0:T(8,128)(2,1)S(1)}, u32[]{:S(2)}, u32[]{:S(2)}) %collective-permute-start.4) | collective-permute-done | bytes 251936 | tf_op jit(solution)/shard_map/ppermute | solution.py:94
  123.1 6.1 %collective-permute-done.5 = bf16[328,384]{1,0:T(8,128)(2,1)S(1)} collective-permute-done((bf16[328,384]{1,0:T(8,128)(2,1)S(1)}, bf16[328,384]{1,0:T(8,128)(2,1)S(1)}, u32[]{:S(2)}, u32[]{:S(2)}) %collective-permute-start.5) | collective-permute-done | bytes 251936 | tf_op jit(solution)/shard_map/ppermute | solution.py:100
  130.4 1.5 collective-permute-start.6
  133.3 4.2 %all-to-all-start.2 = ((bf16[4,96,1,4,2,128]{5,1,4,3,2,0:T(8,128)(2,1)}), bf16[4,96,1,4,2,128]{5,1,4,3,2,0:T(8,128)(2,1)S(1)}, u32[]{:S(2)}, u32[]{:S(2)}) async-start(bf16[4,96,1,4,2,128]{5,1,4,3,2,0:T(8,128)(2,1)} %copy.32), calls=%async_computation.2 | async-start | bytes 1572864 | tf_op jit(solution)/shard_map/all_to_all | solution.py:178
  137.4 4.1 %collective-permute-done.6 = bf16[656,384]{1,0:T(8,128)(2,1)S(1)} collective-permute-done((bf16[656,384]{1,0:T(8,128)(2,1)}, bf16[656,384]{1,0:T(8,128)(2,1)S(1)}, u32[]{:S(2)}, u32[]{:S(2)}) %collective-permute-start.6) | collective-permute-done | bytes 503840 | tf_op jit(solution)/shard_map/ppermute | solution.py:100
  142.0 1.1 pad_maximum_fusion.1
  143.1 11.9 %all-to-all-done.2 = bf16[4,96,1,4,2,128]{5,1,4,3,2,0:T(8,128)(2,1)S(1)} async-done(((bf16[4,96,1,4,2,128]{5,1,4,3,2,0:T(8,128)(2,1)}), bf16[4,96,1,4,2,128]{5,1,4,3,2,0:T(8,128)(2,1)S(1)}, u32[]{:S(2)}, u32[]{:S(2)}) %all-to-all-start.2) | async-done | bytes 786464 | tf_op jit(solution)/shard_map/all_to_all | solution.py:178
  157.1 2.4 %convert.5 = f32[3,3,3,96,384]{4,3,2,1,0:T(8,128)} convert(bf16[3,3,3,96,384]{4,3,2,1,0:T(8,128)(2,1)S(1)} %bitcast.216) | non-fusion elementwise | flops 995328 | bytes 5971968 | tf_op jit(solution)/shard_map/reshape | solution.py:200
  (96 shorter events, 21.3 us)
Async XLA Ops:
  0.6 34.6 %copy-start = (bf16[384,384]{1,0:T(8,128)(2,1)S(1)}, bf16[384,384]{1,0:T(8,128)(2,1)}, u32[]{:S(2)}) copy-start(bf16[384,384]{1,0:T(8,128)(2,1)} %param.19) | copy-start | bytes 884740
  11.0 22.4 %slice-start = ((f32[1152]{0:T(1024)}), f32[384]{0:T(512)S(1)}, s32[]{:S(2)}) async-start(f32[1152]{0:T(1024)} %param.18), calls=%async_computation.3 | async-start | bytes 4096 | tf_op jit(solution)/shard_map/slice | solution.py:140
  11.1 11.8 %all-to-all-start = ((bf16[96,1,4,2,128]{4,0,3,1,2:T(8,128)(2,1)}), bf16[96,1,4,2,128]{4,0,3,1,2:T(8,128)(2,1)S(1)}, u32[]{:S(2)}, u32[]{:S(2)}) async-start(bf16[96,1,4,2,128]{4,0,3,1,2:T(8,128)(2,1)} %fusion.94), calls=%async_computation | async-start | bytes 393216 | tf_op jit(solution)/shard_map/all_to_all | solution.py:132
  24.5 10.8 %copy-start.9 = (f32[384]{0:T(512)S(1)}, f32[384]{0:T(512)}, u32[]{:S(2)}) copy-start(f32[384]{0:T(512)} %param.20) | copy-start | bytes 4612
  35.3 4.9 %copy-start.5 = (bf16[96,1,4,2,128]{4,3,2,1,0:T(2,128)(2,1)S(1)}, bf16[96,1,4,2,128]{4,3,2,1,0:T(2,128)(2,1)}, u32[]{:S(2)}) copy-start(bf16[96,1,4,2,128]{4,3,2,1,0:T(2,128)(2,1)} %param.25) | copy-start | bytes 589828
  35.3 11.2 %copy-start.3 = (bf16[96,1,4,2,128]{4,3,2,1,0:T(2,128)(2,1)S(1)}, bf16[96,1,4,2,128]{4,3,2,1,0:T(2,128)(2,1)}, u32[]{:S(2)}) copy-start(bf16[96,1,4,2,128]{4,3,2,1,0:T(2,128)(2,1)} %param.13) | copy-start | bytes 589828
  35.9 33.9 %copy-start.6 = (f32[96]{0:T(128)S(1)}, f32[96]{0:T(128)}, u32[]{:S(2)}) copy-start(f32[96]{0:T(128)} %param.22) | copy-start | bytes 1156
  35.9 33.9 %copy-start.7 = (f32[96]{0:T(128)S(1)}, f32[96]{0:T(128)}, u32[]{:S(2)}) copy-start(f32[96]{0:T(128)} %param.21) | copy-start | bytes 1156
  36.7 9.7 %all-to-all-start.1 = ((bf16[384,1,1,2,128]{4,3,2,1,0:T(2,128)(2,1)}), bf16[384,1,1,2,128]{4,3,2,1,0:T(2,128)(2,1)S(1)}, u32[]{:S(2)}, u32[]{:S(2)}) async-start(bf16[384,1,1,2,128]{4,3,2,1,0:T(2,128)(2,1)} %copy.28), calls=%async_computation.1 | async-start | bytes 393216 | tf_op jit(solution)/shard_map/all_to_all | solution.py:158
  70.2 6.7 %collective-permute-start = (bf16[96,1,4,1,128]{4,0,3,2,1:T(8,128)(2,1)S(1)}, bf16[96,1,4,1,128]{4,0,3,2,1:T(8,128)(2,1)S(1)}, u32[]{:S(2)}, u32[]{:S(2)}) collective-permute-start(bf16[96,1,4,1,128]{4,0,3,2,1:T(8,128)(2,1)S(1)} %get-tuple-element.65), channel_id=1, source_target_pairs={{0,4},{1,5},{2,6},{3,7},{8,12},{9,13},{10,14},{11,15},{16,20},{17,... | collective-permute-start | bytes 294920 | tf_op jit(solution)/shard_map/ppermute | solution.py:19
  73.7 6.5 %collective-permute-start.1 = (bf16[96,1,4,1,128]{4,0,3,2,1:T(8,128)(2,1)S(1)}, bf16[96,1,4,1,128]{4,0,3,2,1:T(8,128)(2,1)S(1)}, u32[]{:S(2)}, u32[]{:S(2)}) collective-permute-start(bf16[96,1,4,1,128]{4,0,3,2,1:T(8,128)(2,1)S(1)} %get-tuple-element.66), channel_id=1, source_target_pairs={{4,0},{5,1},{6,2},{7,3},{12,8},{13,9},{14,10},{15,11},{20,16},{21,... | collective-permute-start | bytes 294920 | tf_op jit(solution)/shard_map/ppermute | solution.py:20
  85.6 1.3 copy-start.4
  90.7 1.9 %copy-start.1 = (f32[2624,384]{1,0:T(8,128)}, f32[2624,384]{1,0:T(8,128)S(1)}, u32[]{:S(2)}) copy-start(f32[2624,384]{1,0:T(8,128)S(1)} %pad.10) | copy-start | bytes 12091396
  92.7 2.8 %collective-permute-start.2 = (bf16[1312,384]{1,0:T(8,128)(2,1)S(1)}, bf16[1312,384]{1,0:T(8,128)(2,1)}, u32[]{:S(2)}, u32[]{:S(2)}) collective-permute-start(bf16[1312,384]{1,0:T(8,128)(2,1)S(1)} %fusion.47), channel_id=1, source_target_pairs={{0,1},{1,0},{2,3},{3,2},{4,5},{5,4},{6,7},{7,6},{8,9},{9,8},{10,11... | collective-permute-start | bytes 3022856 | tf_op jit(solution)/shard_map/ppermute | solution.py:94
  98.4 13.8 %collective-permute-start.3 = (bf16[656,384]{1,0:T(8,128)(2,1)}, bf16[656,384]{1,0:T(8,128)(2,1)}, u32[]{:S(2)}, u32[]{:S(2)}) collective-permute-start(bf16[656,384]{1,0:T(8,128)(2,1)} %fusion.56), channel_id=1, source_target_pairs={{0,2},{1,3},{2,0},{3,1},{4,6},{5,7},{6,4},{7,5},{8,10},{9,11},{10,... | collective-permute-start | bytes 1511432 | tf_op jit(solution)/shard_map/ppermute | solution.py:94
  113.4 1.0 copy-start.2
  114.4 7.3 %collective-permute-start.4 = (bf16[328,384]{1,0:T(8,128)(2,1)S(1)}, bf16[328,384]{1,0:T(8,128)(2,1)S(1)}, u32[]{:S(2)}, u32[]{:S(2)}) collective-permute-start(bf16[328,384]{1,0:T(8,128)(2,1)S(1)} %fusion.89), channel_id=1, source_target_pairs={{0,4},{4,0},{1,5},{5,1},{2,6},{6,2},{3,7},{7,3},{8,12},{12,8},{9,1... | collective-permute-start | bytes 755720 | tf_op jit(solution)/shard_map/ppermute | solution.py:94
  122.8 6.5 %collective-permute-start.5 = (bf16[328,384]{1,0:T(8,128)(2,1)S(1)}, bf16[328,384]{1,0:T(8,128)(2,1)S(1)}, u32[]{:S(2)}, u32[]{:S(2)}) collective-permute-start(bf16[328,384]{1,0:T(8,128)(2,1)S(1)} %fusion.61), channel_id=1, source_target_pairs={{0,4},{4,0},{1,5},{5,1},{2,6},{6,2},{3,7},{7,3},{8,12},{12,8},{9,1... | collective-permute-start | bytes 755720 | tf_op jit(solution)/shard_map/ppermute | solution.py:100
  130.4 11.2 %collective-permute-start.6 = (bf16[656,384]{1,0:T(8,128)(2,1)}, bf16[656,384]{1,0:T(8,128)(2,1)S(1)}, u32[]{:S(2)}, u32[]{:S(2)}) collective-permute-start(bf16[656,384]{1,0:T(8,128)(2,1)} %get-tuple-element.61), channel_id=1, source_target_pairs={{0,2},{1,3},{2,0},{3,1},{4,6},{5,7},{6,4},{7,5},{8,10},{9,11},{10,... | collective-permute-start | bytes 1511432 | tf_op jit(solution)/shard_map/ppermute | solution.py:100
  133.3 21.7 %all-to-all-start.2 = ((bf16[4,96,1,4,2,128]{5,1,4,3,2,0:T(8,128)(2,1)}), bf16[4,96,1,4,2,128]{5,1,4,3,2,0:T(8,128)(2,1)S(1)}, u32[]{:S(2)}, u32[]{:S(2)}) async-start(bf16[4,96,1,4,2,128]{5,1,4,3,2,0:T(8,128)(2,1)} %copy.32), calls=%async_computation.2 | async-start | bytes 1572864 | tf_op jit(solution)/shard_map/all_to_all | solution.py:178
  141.9 13.2 %copy-start.8 = (f32[96]{0:T(128)S(1)}, f32[96]{0:T(128)}, u32[]{:S(2)}) copy-start(f32[96]{0:T(128)} %param.24) | copy-start | bytes 1156
  143.1 13.0 %collective-permute-start.7 = (bf16[1312,384]{1,0:T(8,128)(2,1)}, bf16[1312,384]{1,0:T(8,128)(2,1)S(1)}, u32[]{:S(2)}, u32[]{:S(2)}) collective-permute-start(bf16[1312,384]{1,0:T(8,128)(2,1)} %get-tuple-element.57), channel_id=1, source_target_pairs={{0,1},{1,0},{2,3},{3,2},{4,5},{5,4},{6,7},{7,6},{8,9},{9,8},{10,11... | collective-permute-start | bytes 3022856 | tf_op jit(solution)/shard_map/ppermute | solution.py:100

commit v4 on v3

--- a/solution.py
+++ b/solution.py
@@ -184,7 +184,9 @@
     masked_cot = cotangent * mask.astype(jnp.bfloat16)[None, :, :, None, None]
     full_width = chans * lax.axis_size("ch")
     carry = jnp.zeros((3, 9 * chans, full_width), jnp.float32)
-    piece = lax.all_gather(masked_cot, "ch", axis=0, tiled=True)
+    copies = jnp.broadcast_to(masked_cot[None], (shares,) + masked_cot.shape)
+    piece = lax.all_to_all(copies, "ch", split_axis=0, concat_axis=0, tiled=True)
+    piece = piece.reshape((shares * chans,) + masked_cot.shape[1:])
     start = jnp.int32(0)
     for time_tap in range(3):
         part = lax.dot_general(

time: 160 us -> 154 us (0.963)
  blocking collectives: 37 us -> 19.7 us
  starting transfers between devices: 21.6 us -> 26.1 us
  local copies, waits for them, and re-layouts: 12.9 us -> 16.7 us
  other arithmetic: 15.6 us -> 19.1 us
  waiting for transfers between devices: 59.5 us -> 57.1 us
    all_gather x1 -> x0, blocking collectives: 17.3 us -> none  [body(): piece = lax.all_gather(masked_cot, 'ch', axis=0, tiled=True)]
    all_to_all x0 -> x1, starting transfers between devices: none -> 3.49 us  [body(): lax.all_to_all(copies, 'ch', split_axis=0, concat_axis=0, tiled=True)]
    squeeze x3, other arithmetic: 1.45 us -> 3.7 us  [butterfly_sum(): first = lax.dynamic_index_in_dim(pair, side, keepdims=False)]
    unnamed x29 -> x39, local copies, waits for them, and re-layouts: 5.27 us -> 5.94 us
  transfers between devices with their start and end apart: 11 -> 12, of which waited for: 9 -> 9; matrix products, arithmetic and copies ran while one was open for 4% -> 10% of each run, Pallas kernels for 0% -> 0%
where the time goes in v4:
time: 154 us; the launch traced here: 153 us
  waiting for transfers between devices  57.1 us (37%)
  starting transfers between devices  26.1 us (17%)
  blocking collectives  19.7 us (13%)
  other arithmetic  19.1 us (12%)
  local copies, waits for them, and re-layouts  16.7 us (11%)
  matrix products  12.6 us (8%)
  between operations  1.86 us (1%)
    ppermute x3, waiting for transfers between devices, butterfly_sum(): got = lax.ppermute(send.astype(jnp.bfloat16), axis, perm)  22.1 us
    all_to_all x1, waiting for transfers between devices, body(): parts = lax.all_to_all(parts, 'ch', split_axis=0, concat_axis=0, tiled=True)  11.7 us
    psum x2, blocking collectives, body(): first, second = lax.psum((first, second), 'ha')  10.8 us
    ppermute x3, waiting for transfers between devices, butterfly_sum(): got = lax.ppermute(work, axis, perm)  9.43 us
    all_gather x1, blocking collectives, body(): piece = lax.all_gather(pairs, 'ha', axis=1, tiled=True)  8.94 us
    unnamed x39, local copies, waits for them, and re-layouts  5.94 us
    all_to_all x1, waiting for transfers between devices, body(): lax.all_to_all(projected, 'ch', split_axis=0, concat_axis=2, tiled=True)  5.89 us
    all_to_all x1, waiting for transfers between devices, body(): lax.all_to_all(normed, 'ch', split_axis=2, concat_axis=0, tiled=True)  5.55 us
  transfers between devices with their start and end apart: 12, of which 9 were waited for; matrix products, arithmetic and copies ran while one was open for 10% of the time, Pallas kernels for 0%

profile of v4, /device:TPU:0, one launch (start us, length us, event | category | flops | bytes accessed | tf_op | source)
XLA Modules:
  0.0 153.2 jit_solution(3477653646799306401)
XLA Ops:
  3.1 5.9 %all-reduce.4 = (f32[8,1]{0,1:T(1,128)S(1)}, f32[8,1]{0,1:T(1,128)S(1)}) all-reduce(f32[8,1]{0,1:T(1,128)S(1)} %convolution_bitcast_fusion.3, f32[8,1]{0,1:T(1,128)S(1)} %convolution_bitcast_fusion.2), channel_id=1, replica_groups=mesh['ch'=4,'ha'=2,'dp'=4] {'ha'}, use_global_device_ids=true, to_apply=%region_2.0 | all-reduce | flops 16 | bytes 128 | tf_op jit(solution)/shard_map/psum | solution.py:128
  9.2 1.8 %fusion.91 = bf16[96,1,4,2,128]{4,0,3,1,2:T(8,128)(2,1)} fusion(f32[96]{0:T(128)} %param.16, f32[96]{0:T(128)} %param.15, f32[96]{0:T(128)S(1)} %mul.117, f32[96]{0:T(128)S(1)} %sub.78, bf16[96,1,4,2,128]{4,3,2,1,0:T(2,128)(2,1)} %param.13), kind=kLoop, calls=%fused_computation.119 | loop fusion | flops 589824 | bytes 394752 | tf_op jit(solution)/shard_map/convert_element_type | solution.py:129
  11.1 5.5 %all-to-all-start = ((bf16[96,1,4,2,128]{4,0,3,1,2:T(8,128)(2,1)}), bf16[96,1,4,2,128]{4,0,3,1,2:T(8,128)(2,1)S(1)}, u32[]{:S(2)}, u32[]{:S(2)}) async-start(bf16[96,1,4,2,128]{4,0,3,1,2:T(8,128)(2,1)} %fusion.91), calls=%async_computation | async-start | bytes 393216 | tf_op jit(solution)/shard_map/all_to_all | solution.py:132
  17.3 5.5 %all-to-all-done = bf16[96,1,4,2,128]{4,0,3,1,2:T(8,128)(2,1)S(1)} async-done(((bf16[96,1,4,2,128]{4,0,3,1,2:T(8,128)(2,1)}), bf16[96,1,4,2,128]{4,0,3,1,2:T(8,128)(2,1)S(1)}, u32[]{:S(2)}, u32[]{:S(2)}) %all-to-all-start) | async-done | bytes 196640 | tf_op jit(solution)/shard_map/all_to_all | solution.py:132
  23.0 1.5 fusion.37
  24.5 8.9 %all-gather = bf16[512,768]{1,0:T(8,128)(2,1)S(1)} all-gather(bf16[256,768]{1,0:T(8,128)(2,1)S(1)} %fusion.37), channel_id=2, replica_groups=mesh['ch'=4,'ha'=2,'dp'=4] {'ha'}, dimensions={0}, use_global_device_ids=true | all-gather | bytes 1179648 | tf_op jit(solution)/shard_map/all_gather | solution.py:151
  33.4 1.6 %fusion.119 = (f32[256]{0:T(256)S(1)}, f32[256,512]{1,0:T(8,128)S(1)}) fusion(bf16[1,512,768]{2,1,0:T(8,128)(2,1)S(1)} %bitcast.223, bf16[384,1152]{1,0:T(8,128)(2,1)} %param.17, f32[384]{0:T(512)S(1)} %slice-done, bf16[48,8,2,128]{3,2,1,0:T(2,128)(2,1)S(1)} %bitcast.232), kind=kOutput, calls=%fused_computation.180 | convolution fusion | flops 176619264 | bytes 1412096 | tf_op jit(solution)/shard_map/itc,isc->its/dot_general | solution.py:51
  36.7 3.4 %all-to-all-start.1 = ((bf16[384,1,1,2,128]{4,3,2,1,0:T(2,128)(2,1)}), bf16[384,1,1,2,128]{4,3,2,1,0:T(2,128)(2,1)S(1)}, u32[]{:S(2)}, u32[]{:S(2)}) async-start(bf16[384,1,1,2,128]{4,3,2,1,0:T(2,128)(2,1)} %copy.28), calls=%async_computation.1 | async-start | bytes 393216 | tf_op jit(solution)/shard_map/all_to_all | solution.py:158
  40.4 5.9 %all-to-all-done.1 = bf16[384,1,1,2,128]{4,3,2,1,0:T(2,128)(2,1)S(1)} async-done(((bf16[384,1,1,2,128]{4,3,2,1,0:T(2,128)(2,1)}), bf16[384,1,1,2,128]{4,3,2,1,0:T(2,128)(2,1)S(1)}, u32[]{:S(2)}, u32[]{:S(2)}) %all-to-all-start.1) | async-done | bytes 196640 | tf_op jit(solution)/shard_map/all_to_all | solution.py:158
  48.2 3.5 %all-to-all-start.3 = ((bf16[4,96,1,4,2,128]{5,1,4,3,2,0:T(8,128)(2,1)}), bf16[4,96,1,4,2,128]{5,1,4,3,2,0:T(8,128)(2,1)S(1)}, u32[]{:S(2)}, u32[]{:S(2)}) async-start(bf16[4,96,1,4,2,128]{5,1,4,3,2,0:T(8,128)(2,1)} %broadcast_in_dim.17), calls=%async_computation.3 | async-start | bytes 1572864 | tf_op jit(solution)/shard_map/all_to_all | solution.py:188
  51.7 4.9 %all-reduce.3 = (f32[8,1]{0,1:T(1,128)S(1)}, f32[8,1]{0,1:T(1,128)S(1)}) all-reduce(f32[8,1]{0,1:T(1,128)S(1)} %convolution_bitcast_fusion.1, f32[8,1]{0,1:T(1,128)S(1)} %convolution_bitcast_fusion), channel_id=1, replica_groups=mesh['ch'=4,'ha'=2,'dp'=4] {'ha'}, use_global_device_ids=true, to_apply=%region_10.11 | all-reduce | flops 16 | bytes 128 | tf_op jit(solution)/shard_map/psum | solution.py:161
  57.3 3.5 %collective-permute-start = (bf16[96,1,4,1,128]{4,0,3,2,1:T(8,128)(2,1)S(1)}, bf16[96,1,4,1,128]{4,0,3,2,1:T(8,128)(2,1)S(1)}, u32[]{:S(2)}, u32[]{:S(2)}) collective-permute-start(bf16[96,1,4,1,128]{4,0,3,2,1:T(8,128)(2,1)S(1)} %get-tuple-element.65), channel_id=1, source_target_pairs={{0,4},{1,5},{2,6},{3,7},{8,12},{9,13},{10,14},{11,15},{16,20},{17,... | collective-permute-start | bytes 294920 | tf_op jit(solution)/shard_map/ppermute | solution.py:19
  60.8 1.5 collective-permute-start.1
  62.3 2.6 %fusion.117 = (bf16[1,3,3,96,384]{4,3,2,1,0:T(8,128)(2,1)}, bf16[1,3,3,96,384]{4,3,2,1,0:T(8,128)(2,1)S(1)}, bf16[1,3,3,96,384]{4,3,2,1,0:T(8,128)(2,1)S(1)}) fusion(bf16[3,3,3,96,384]{4,3,2,1,0:T(8,128)(2,1)} %param.23), kind=kLoop, calls=%fused_computation.178 | loop fusion | bytes 3981312 | tf_op jit(solution)/shard_map/slice | solution.py:171
  64.9 2.4 %collective-permute-done.1 = bf16[96,1,4,1,128]{4,0,3,2,1:T(8,128)(2,1)S(1)} collective-permute-done((bf16[96,1,4,1,128]{4,0,3,2,1:T(8,128)(2,1)S(1)}, bf16[96,1,4,1,128]{4,0,3,2,1:T(8,128)(2,1)S(1)}, u32[]{:S(2)}, u32[]{:S(2)}) %collective-permute-start.1) | collective-permute-done | bytes 98336 | tf_op jit(solution)/shard_map/ppermute | solution.py:20
  72.8 1.3 fusion.34
  74.1 2.6 %fusion.19 = f32[1,864,384]{2,1,0:T(8,128)S(1)} fusion(bf16[384,4,2,128]{3,0,2,1:T(8,128)(2,1)S(1)} %bitcast.225, bf16[864,1,4,2,128]{4,0,3,2,1:T(8,128)(2,1)} %copy-done.7), kind=kOutput, calls=%fused_computation.29 | convolution fusion | flops 679477248 | bytes 3883008 | tf_op jit(solution)/shard_map/dot_general | solution.py:192
  81.0 1.9 %copy-done.1 = f32[2624,384]{1,0:T(8,128)} copy-done((f32[2624,384]{1,0:T(8,128)}, f32[2624,384]{1,0:T(8,128)S(1)}, u32[]{:S(2)}) %copy-start.1) | copy-done | bytes 4030488
  83.1 2.7 %collective-permute-done.2 = bf16[1312,384]{1,0:T(8,128)(2,1)} collective-permute-done((bf16[1312,384]{1,0:T(8,128)(2,1)S(1)}, bf16[1312,384]{1,0:T(8,128)(2,1)}, u32[]{:S(2)}, u32[]{:S(2)}) %collective-permute-start.2) | collective-permute-done | bytes 1007648 | tf_op jit(solution)/shard_map/ppermute | solution.py:94
  85.8 2.0 %bitcast_add_fusion = f32[1312,384]{1,0:T(8,128)S(1)} fusion(bf16[1312,384]{1,0:T(8,128)(2,1)} %collective-permute-done.2, f32[2,1312,384]{2,1,0:T(8,128)} %bitcast.214, s32[]{:T(128)S(6)} %select_n.30), kind=kLoop, calls=%fused_computation.12 | loop fusion | flops 1007616 | bytes 5038084 | tf_op jit(solution)/shard_map/add | solution.py:95
  88.7 1.5 collective-permute-start.3
  90.2 12.3 %collective-permute-done.3 = bf16[656,384]{1,0:T(8,128)(2,1)} collective-permute-done((bf16[656,384]{1,0:T(8,128)(2,1)}, bf16[656,384]{1,0:T(8,128)(2,1)}, u32[]{:S(2)}, u32[]{:S(2)}) %collective-permute-start.3) | collective-permute-done | bytes 503840 | tf_op jit(solution)/shard_map/ppermute | solution.py:94
  102.6 2.1 %bitcast_add_fusion.1 = f32[656,384]{1,0:T(8,128)} fusion(bf16[656,384]{1,0:T(8,128)(2,1)} %collective-permute-done.3, f32[2,656,384]{2,1,0:T(8,128)S(1)} %bitcast.217, s32[]{:T(128)S(6)} %select_n.32), kind=kLoop, calls=%fused_computation.64 | loop fusion | flops 503808 | bytes 2519044 | tf_op jit(solution)/shard_map/add | solution.py:95
  106.0 7.1 %collective-permute-done.4 = bf16[328,384]{1,0:T(8,128)(2,1)S(1)} collective-permute-done((bf16[328,384]{1,0:T(8,128)(2,1)S(1)}, bf16[328,384]{1,0:T(8,128)(2,1)S(1)}, u32[]{:S(2)}, u32[]{:S(2)}) %collective-permute-start.4) | collective-permute-done | bytes 251936 | tf_op jit(solution)/shard_map/ppermute | solution.py:94
  114.5 6.1 %collective-permute-done.5 = bf16[328,384]{1,0:T(8,128)(2,1)S(1)} collective-permute-done((bf16[328,384]{1,0:T(8,128)(2,1)S(1)}, bf16[328,384]{1,0:T(8,128)(2,1)S(1)}, u32[]{:S(2)}, u32[]{:S(2)}) %collective-permute-start.5) | collective-permute-done | bytes 251936 | tf_op jit(solution)/shard_map/ppermute | solution.py:100
  121.9 1.5 %collective-permute-start.6 = (bf16[656,384]{1,0:T(8,128)(2,1)}, bf16[656,384]{1,0:T(8,128)(2,1)}, u32[]{:S(2)}, u32[]{:S(2)}) collective-permute-start(bf16[656,384]{1,0:T(8,128)(2,1)} %get-tuple-element.61), channel_id=1, source_target_pairs={{0,2},{1,3},{2,0},{3,1},{4,6},{5,7},{6,4},{7,5},{8,10},{9,11},{10,... | collective-permute-start | bytes 1511432 | tf_op jit(solution)/shard_map/ppermute | solution.py:100
  124.8 5.0 %all-to-all-start.2 = ((bf16[4,96,1,4,2,128]{5,1,4,3,2,0:T(8,128)(2,1)}), bf16[4,96,1,4,2,128]{5,1,4,3,2,0:T(8,128)(2,1)S(1)}, u32[]{:S(2)}, u32[]{:S(2)}) async-start(bf16[4,96,1,4,2,128]{5,1,4,3,2,0:T(8,128)(2,1)} %copy.32), calls=%async_computation.2 | async-start | bytes 1572864 | tf_op jit(solution)/shard_map/all_to_all | solution.py:178
  129.9 3.3 %collective-permute-done.6 = bf16[656,384]{1,0:T(8,128)(2,1)} collective-permute-done((bf16[656,384]{1,0:T(8,128)(2,1)}, bf16[656,384]{1,0:T(8,128)(2,1)}, u32[]{:S(2)}, u32[]{:S(2)}) %collective-permute-start.6) | collective-permute-done | bytes 503840 | tf_op jit(solution)/shard_map/ppermute | solution.py:100
  133.2 1.5 fusion.57
  135.8 11.7 %all-to-all-done.2 = bf16[4,96,1,4,2,128]{5,1,4,3,2,0:T(8,128)(2,1)S(1)} async-done(((bf16[4,96,1,4,2,128]{5,1,4,3,2,0:T(8,128)(2,1)}), bf16[4,96,1,4,2,128]{5,1,4,3,2,0:T(8,128)(2,1)S(1)}, u32[]{:S(2)}, u32[]{:S(2)}) %all-to-all-start.2) | async-done | bytes 786464 | tf_op jit(solution)/shard_map/all_to_all | solution.py:178
  148.5 2.0 %fusion.51 = (bf16[1312,384]{1,0:T(8,128)(2,1)S(1)}, bf16[1312,384]{1,0:T(8,128)(2,1)S(1)}) fusion(s32[]{:T(128)S(6)} %select_n.30, bf16[1,1312,384]{2,1,0:T(8,128)(2,1)S(1)} %get-tuple-element.58, bf16[1,1312,384]{2,1,0:T(8,128)(2,1)} %bitcast.78, s32[]{:T(128)S(6)} %select_n.31), kind=kLoop, calls=%fused_computation.62 | loop fusion | flops 1007616 | bytes 4030472 | tf_op jit(solution)/shard_map/jit(dynamic_index_in_dim)/squeeze | solution.py:102
  150.8 2.4 %convert.5 = f32[3,3,3,96,384]{4,3,2,1,0:T(8,128)} convert(bf16[3,3,3,96,384]{4,3,2,1,0:T(8,128)(2,1)S(1)} %bitcast.215) | non-fusion elementwise | flops 995328 | bytes 5971968 | tf_op jit(solution)/shard_map/reshape | solution.py:202
  (110 shorter events, 25.9 us)
Async XLA Ops:
  0.6 34.6 %copy-start = (bf16[384,384]{1,0:T(8,128)(2,1)S(1)}, bf16[384,384]{1,0:T(8,128)(2,1)}, u32[]{:S(2)}) copy-start(bf16[384,384]{1,0:T(8,128)(2,1)} %param.19) | copy-start | bytes 884740
  11.0 22.4 %slice-start = ((f32[1152]{0:T(1024)}), f32[384]{0:T(512)S(1)}, s32[]{:S(2)}) async-start(f32[1152]{0:T(1024)} %param.18), calls=%async_computation.4 | async-start | bytes 4096 | tf_op jit(solution)/shard_map/slice | solution.py:140
  11.1 11.8 %all-to-all-start = ((bf16[96,1,4,2,128]{4,0,3,1,2:T(8,128)(2,1)}), bf16[96,1,4,2,128]{4,0,3,1,2:T(8,128)(2,1)S(1)}, u32[]{:S(2)}, u32[]{:S(2)}) async-start(bf16[96,1,4,2,128]{4,0,3,1,2:T(8,128)(2,1)} %fusion.91), calls=%async_computation | async-start | bytes 393216 | tf_op jit(solution)/shard_map/all_to_all | solution.py:132
  24.5 10.8 %copy-start.14 = (f32[384]{0:T(512)S(1)}, f32[384]{0:T(512)}, u32[]{:S(2)}) copy-start(f32[384]{0:T(512)} %param.20) | copy-start | bytes 4612
  35.3 4.8 %copy-start.10 = (bf16[96,1,4,2,128]{4,3,2,1,0:T(2,128)(2,1)S(1)}, bf16[96,1,4,2,128]{4,3,2,1,0:T(2,128)(2,1)}, u32[]{:S(2)}) copy-start(bf16[96,1,4,2,128]{4,3,2,1,0:T(2,128)(2,1)} %param.25) | copy-start | bytes 589828
  35.3 11.1 %copy-start.9 = (bf16[96,1,4,2,128]{4,3,2,1,0:T(2,128)(2,1)S(1)}, bf16[96,1,4,2,128]{4,3,2,1,0:T(2,128)(2,1)}, u32[]{:S(2)}) copy-start(bf16[96,1,4,2,128]{4,3,2,1,0:T(2,128)(2,1)} %param.13) | copy-start | bytes 589828
  36.7 9.6 %all-to-all-start.1 = ((bf16[384,1,1,2,128]{4,3,2,1,0:T(2,128)(2,1)}), bf16[384,1,1,2,128]{4,3,2,1,0:T(2,128)(2,1)S(1)}, u32[]{:S(2)}, u32[]{:S(2)}) async-start(bf16[384,1,1,2,128]{4,3,2,1,0:T(2,128)(2,1)} %copy.28), calls=%async_computation.1 | async-start | bytes 393216 | tf_op jit(solution)/shard_map/all_to_all | solution.py:158
  40.4 16.6 %copy-start.11 = (f32[96]{0:T(128)S(1)}, f32[96]{0:T(128)}, u32[]{:S(2)}) copy-start(f32[96]{0:T(128)} %param.22) | copy-start | bytes 1156
  40.4 16.6 %copy-start.12 = (f32[96]{0:T(128)S(1)}, f32[96]{0:T(128)}, u32[]{:S(2)}) copy-start(f32[96]{0:T(128)} %param.21) | copy-start | bytes 1156
  48.2 25.9 %all-to-all-start.3 = ((bf16[4,96,1,4,2,128]{5,1,4,3,2,0:T(8,128)(2,1)}), bf16[4,96,1,4,2,128]{5,1,4,3,2,0:T(8,128)(2,1)S(1)}, u32[]{:S(2)}, u32[]{:S(2)}) async-start(bf16[4,96,1,4,2,128]{5,1,4,3,2,0:T(8,128)(2,1)} %broadcast_in_dim.17), calls=%async_computation.3 | async-start | bytes 1572864 | tf_op jit(solution)/shard_map/all_to_all | solution.py:188
  57.3 7.5 %collective-permute-start = (bf16[96,1,4,1,128]{4,0,3,2,1:T(8,128)(2,1)S(1)}, bf16[96,1,4,1,128]{4,0,3,2,1:T(8,128)(2,1)S(1)}, u32[]{:S(2)}, u32[]{:S(2)}) collective-permute-start(bf16[96,1,4,1,128]{4,0,3,2,1:T(8,128)(2,1)S(1)} %get-tuple-element.65), channel_id=1, source_target_pairs={{0,4},{1,5},{2,6},{3,7},{8,12},{9,13},{10,14},{11,15},{16,20},{17,... | collective-permute-start | bytes 294920 | tf_op jit(solution)/shard_map/ppermute | solution.py:19
  60.8 6.5 %collective-permute-start.1 = (bf16[96,1,4,1,128]{4,0,3,2,1:T(8,128)(2,1)S(1)}, bf16[96,1,4,1,128]{4,0,3,2,1:T(8,128)(2,1)S(1)}, u32[]{:S(2)}, u32[]{:S(2)}) collective-permute-start(bf16[96,1,4,1,128]{4,0,3,2,1:T(8,128)(2,1)S(1)} %get-tuple-element.66), channel_id=1, source_target_pairs={{4,0},{5,1},{6,2},{7,3},{12,8},{13,9},{14,10},{15,11},{20,16},{21,... | collective-permute-start | bytes 294920 | tf_op jit(solution)/shard_map/ppermute | solution.py:20
  69.1 1.2 copy-start.2
  70.0 1.5 copy-start.5
  70.0 2.7 %copy-start.7 = (bf16[864,1,4,2,128]{4,0,3,2,1:T(8,128)(2,1)}, bf16[864,1,4,2,128]{4,0,3,2,1:T(8,128)(2,1)S(1)}, u32[]{:S(2)}) copy-start(bf16[864,1,4,2,128]{4,0,3,2,1:T(8,128)(2,1)S(1)} %get-tuple-element.7) | copy-start | bytes 5308420
  70.3 2.5 %copy-start.3 = (bf16[864,1,4,2,128]{4,0,3,2,1:T(8,128)(2,1)}, bf16[864,1,4,2,128]{4,0,3,2,1:T(8,128)(2,1)S(1)}, u32[]{:S(2)}) copy-start(bf16[864,1,4,2,128]{4,0,3,2,1:T(8,128)(2,1)S(1)} %slice_dynamic-update-slice_fusion) | copy-start | bytes 5308420
  76.7 1.5 copy-start.6
  78.2 1.5 copy-start.4
  81.0 1.9 %copy-start.1 = (f32[2624,384]{1,0:T(8,128)}, f32[2624,384]{1,0:T(8,128)S(1)}, u32[]{:S(2)}) copy-start(f32[2624,384]{1,0:T(8,128)S(1)} %pad.10) | copy-start | bytes 12091396
  83.0 2.8 %collective-permute-start.2 = (bf16[1312,384]{1,0:T(8,128)(2,1)S(1)}, bf16[1312,384]{1,0:T(8,128)(2,1)}, u32[]{:S(2)}, u32[]{:S(2)}) collective-permute-start(bf16[1312,384]{1,0:T(8,128)(2,1)S(1)} %fusion.47), channel_id=1, source_target_pairs={{0,1},{1,0},{2,3},{3,2},{4,5},{5,4},{6,7},{7,6},{8,9},{9,8},{10,11... | collective-permute-start | bytes 3022856 | tf_op jit(solution)/shard_map/ppermute | solution.py:94
  88.7 13.8 %collective-permute-start.3 = (bf16[656,384]{1,0:T(8,128)(2,1)}, bf16[656,384]{1,0:T(8,128)(2,1)}, u32[]{:S(2)}, u32[]{:S(2)}) collective-permute-start(bf16[656,384]{1,0:T(8,128)(2,1)} %fusion.53), channel_id=1, source_target_pairs={{0,2},{1,3},{2,0},{3,1},{4,6},{5,7},{6,4},{7,5},{8,10},{9,11},{10,... | collective-permute-start | bytes 1511432 | tf_op jit(solution)/shard_map/ppermute | solution.py:94
  105.7 7.3 %collective-permute-start.4 = (bf16[328,384]{1,0:T(8,128)(2,1)S(1)}, bf16[328,384]{1,0:T(8,128)(2,1)S(1)}, u32[]{:S(2)}, u32[]{:S(2)}) collective-permute-start(bf16[328,384]{1,0:T(8,128)(2,1)S(1)} %fusion.86), channel_id=1, source_target_pairs={{0,4},{4,0},{1,5},{5,1},{2,6},{6,2},{3,7},{7,3},{8,12},{12,8},{9,1... | collective-permute-start | bytes 755720 | tf_op jit(solution)/shard_map/ppermute | solution.py:94
  114.1 6.5 %collective-permute-start.5 = (bf16[328,384]{1,0:T(8,128)(2,1)S(1)}, bf16[328,384]{1,0:T(8,128)(2,1)S(1)}, u32[]{:S(2)}, u32[]{:S(2)}) collective-permute-start(bf16[328,384]{1,0:T(8,128)(2,1)S(1)} %fusion.58), channel_id=1, source_target_pairs={{0,4},{4,0},{1,5},{5,1},{2,6},{6,2},{3,7},{7,3},{8,12},{12,8},{9,1... | collective-permute-start | bytes 755720 | tf_op jit(solution)/shard_map/ppermute | solution.py:100
  121.9 11.3 %collective-permute-start.6 = (bf16[656,384]{1,0:T(8,128)(2,1)}, bf16[656,384]{1,0:T(8,128)(2,1)}, u32[]{:S(2)}, u32[]{:S(2)}) collective-permute-start(bf16[656,384]{1,0:T(8,128)(2,1)} %get-tuple-element.61), channel_id=1, source_target_pairs={{0,2},{1,3},{2,0},{3,1},{4,6},{5,7},{6,4},{7,5},{8,10},{9,11},{10,... | collective-permute-start | bytes 1511432 | tf_op jit(solution)/shard_map/ppermute | solution.py:100
  123.8 9.4 %copy-start.8 = (bf16[1,656,384]{2,1,0:T(8,128)(2,1)S(1)}, bf16[1,656,384]{2,1,0:T(8,128)(2,1)}, u32[]{:S(2)}) copy-start(bf16[1,656,384]{2,1,0:T(8,128)(2,1)} %get-tuple-element.62) | copy-start | bytes 1511428
  124.8 22.6 %all-to-all-start.2 = ((bf16[4,96,1,4,2,128]{5,1,4,3,2,0:T(8,128)(2,1)}), bf16[4,96,1,4,2,128]{5,1,4,3,2,0:T(8,128)(2,1)S(1)}, u32[]{:S(2)}, u32[]{:S(2)}) async-start(bf16[4,96,1,4,2,128]{5,1,4,3,2,0:T(8,128)(2,1)} %copy.32), calls=%async_computation.2 | async-start | bytes 1572864 | tf_op jit(solution)/shard_map/all_to_all | solution.py:178
  134.6 12.9 %copy-start.13 = (f32[96]{0:T(128)S(1)}, f32[96]{0:T(128)}, u32[]{:S(2)}) copy-start(f32[96]{0:T(128)} %param.24) | copy-start | bytes 1156
  135.7 12.8 %collective-permute-start.7 = (bf16[1312,384]{1,0:T(8,128)(2,1)}, bf16[1312,384]{1,0:T(8,128)(2,1)}, u32[]{:S(2)}, u32[]{:S(2)}) collective-permute-start(bf16[1312,384]{1,0:T(8,128)(2,1)} %get-tuple-element.57), channel_id=1, source_target_pairs={{0,1},{1,0},{2,3},{3,2},{4,5},{5,4},{6,7},{7,6},{8,9},{9,8},{10,11... | collective-permute-start | bytes 3022856 | tf_op jit(solution)/shard_map/ppermute | solution.py:100

commit v5 on v4

--- a/solution.py
+++ b/solution.py
@@ -198,6 +198,7 @@
         carry = lax.dynamic_update_slice(
             carry, part[None], (jnp.int32(time_tap), jnp.int32(0), start)
         )
+    parts, carry = lax.optimization_barrier((parts, carry))
     weight_grad = butterfly_sum(carry.reshape(27 * chans, full_width), ("dp", "ha"))
     weight_grad = weight_grad.reshape(3, 3, 3, chans, full_width)
     return (mixed, weight_grad)

time: 154 us -> 155 us (level)
  other arithmetic: 19.1 us -> 15 us
  matrix products: 12.6 us -> 14.8 us
  local copies, waits for them, and re-layouts: 16.7 us -> 18.5 us
    all_to_all x1, waiting for transfers between devices: 11.7 us -> 3.9 us  [body(): parts = lax.all_to_all(parts, 'ch', split_axis=0, concat_axis=0, tiled=True)]
    ppermute x3, waiting for transfers between devices: 9.43 us -> 16.8 us  [butterfly_sum(): got = lax.ppermute(work, axis, perm)]
    squeeze x3, other arithmetic: 3.7 us -> 1.45 us  [butterfly_sum(): first = lax.dynamic_index_in_dim(pair, side, keepdims=False)]
    dot_general x3, matrix products: 4.77 us -> 6.91 us  [body(): lax.dot_general(stacks[time_tap], piece, (((1, 2, 3, 4), (1, 2, 3, 4)), (...]
    pad x1, local copies, waits for them, and re-layouts: 0.26 us -> 2.39 us  [butterfly_sum(): work = jnp.pad(table, ((0, padded - length), (0, 0)))]
    dynamic_update_slice x1, local copies, waits for them, and re-layouts: 0.26 us -> 2.2 us  [body(): lax.dynamic_update_slice(carry, part[None], (jnp.int32(time_tap), jnp.int...]
    concatenate x3, other arithmetic: 2.37 us -> 0.47 us  [butterfly_sum(): work = jnp.concatenate([first, second], axis=0)]
    unnamed x39 -> x35, local copies, waits for them, and re-layouts: 5.94 us -> 4.63 us
  transfers between devices with their start and end apart: 12 -> 12, of which waited for: 9 -> 10; matrix products, arithmetic and copies ran while one was open for 10% -> 14% of each run, Pallas kernels for 0% -> 0%
where the time goes in v5:
time: 155 us; the launch traced here: 154 us
  waiting for transfers between devices  57.9 us (37%)
  starting transfers between devices  25.9 us (17%)
  blocking collectives  19.7 us (13%)
  local copies, waits for them, and re-layouts  18.5 us (12%)
  other arithmetic  15 us (10%)
  matrix products  14.8 us (10%)
  between operations  1.84 us (1%)
    ppermute x3, waiting for transfers between devices, butterfly_sum(): got = lax.ppermute(send.astype(jnp.bfloat16), axis, perm)  22.3 us
    ppermute x3, waiting for transfers between devices, butterfly_sum(): got = lax.ppermute(work, axis, perm)  16.8 us
    psum x2, blocking collectives, body(): first, second = lax.psum((first, second), 'ha')  10.8 us
    all_gather x1, blocking collectives, body(): piece = lax.all_gather(pairs, 'ha', axis=1, tiled=True)  8.94 us
    dot_general x3, matrix products, body(): lax.dot_general(stacks[time_tap], piece, (((1, 2, 3, 4), (1, 2, 3, 4)), (...  6.91 us
    all_to_all x1, waiting for transfers between devices, body(): lax.all_to_all(projected, 'ch', split_axis=0, concat_axis=2, tiled=True)  5.89 us
    all_to_all x1, waiting for transfers between devices, body(): lax.all_to_all(normed, 'ch', split_axis=2, concat_axis=0, tiled=True)  5.55 us
    all_to_all x1, starting transfers between devices, body(): lax.all_to_all(normed, 'ch', split_axis=2, concat_axis=0, tiled=True)  5.54 us
  transfers between devices with their start and end apart: 12, of which 10 were waited for; matrix products, arithmetic and copies ran while one was open for 14% of the time, Pallas kernels for 0%

profile of v5, /device:TPU:0, one launch (start us, length us, event | category | flops | bytes accessed | tf_op | source)
XLA Modules:
  0.0 153.6 jit_solution(434818455309339287)
XLA Ops:
  3.1 5.9 %all-reduce.4 = (f32[8,1]{0,1:T(1,128)S(1)}, f32[8,1]{0,1:T(1,128)S(1)}) all-reduce(f32[8,1]{0,1:T(1,128)S(1)} %convolution_bitcast_fusion.3, f32[8,1]{0,1:T(1,128)S(1)} %convolution_bitcast_fusion.2), channel_id=1, replica_groups=mesh['ch'=4,'ha'=2,'dp'=4] {'ha'}, use_global_device_ids=true, to_apply=%region_2.0 | all-reduce | flops 16 | bytes 128 | tf_op jit(solution)/shard_map/psum | solution.py:128
  9.2 1.8 %fusion.91 = bf16[96,1,4,2,128]{4,0,3,1,2:T(8,128)(2,1)} fusion(f32[96]{0:T(128)} %param.16, f32[96]{0:T(128)} %param.15, f32[96]{0:T(128)S(1)} %mul.117, f32[96]{0:T(128)S(1)} %sub.78, bf16[96,1,4,2,128]{4,3,2,1,0:T(2,128)(2,1)} %param.13), kind=kLoop, calls=%fused_computation.119 | loop fusion | flops 589824 | bytes 394752 | tf_op jit(solution)/shard_map/convert_element_type | solution.py:129
  11.1 5.5 %all-to-all-start = ((bf16[96,1,4,2,128]{4,0,3,1,2:T(8,128)(2,1)}), bf16[96,1,4,2,128]{4,0,3,1,2:T(8,128)(2,1)S(1)}, u32[]{:S(2)}, u32[]{:S(2)}) async-start(bf16[96,1,4,2,128]{4,0,3,1,2:T(8,128)(2,1)} %fusion.91), calls=%async_computation | async-start | bytes 393216 | tf_op jit(solution)/shard_map/all_to_all | solution.py:132
  17.3 5.5 %all-to-all-done = bf16[96,1,4,2,128]{4,0,3,1,2:T(8,128)(2,1)S(1)} async-done(((bf16[96,1,4,2,128]{4,0,3,1,2:T(8,128)(2,1)}), bf16[96,1,4,2,128]{4,0,3,1,2:T(8,128)(2,1)S(1)}, u32[]{:S(2)}, u32[]{:S(2)}) %all-to-all-start) | async-done | bytes 196640 | tf_op jit(solution)/shard_map/all_to_all | solution.py:132
  23.0 1.5 fusion.37
  24.5 8.9 %all-gather = bf16[512,768]{1,0:T(8,128)(2,1)S(1)} all-gather(bf16[256,768]{1,0:T(8,128)(2,1)S(1)} %fusion.37), channel_id=2, replica_groups=mesh['ch'=4,'ha'=2,'dp'=4] {'ha'}, dimensions={0}, use_global_device_ids=true | all-gather | bytes 1179648 | tf_op jit(solution)/shard_map/all_gather | solution.py:151
  33.4 1.6 %fusion.119 = (f32[256]{0:T(256)S(1)}, f32[256,512]{1,0:T(8,128)S(1)}) fusion(bf16[1,512,768]{2,1,0:T(8,128)(2,1)S(1)} %bitcast.223, bf16[384,1152]{1,0:T(8,128)(2,1)} %param.17, f32[384]{0:T(512)S(1)} %slice-done, bf16[48,8,2,128]{3,2,1,0:T(2,128)(2,1)S(1)} %bitcast.233), kind=kOutput, calls=%fused_computation.180 | convolution fusion | flops 176619264 | bytes 1412096 | tf_op jit(solution)/shard_map/itc,isc->its/dot_general | solution.py:51
  36.7 3.4 %all-to-all-start.1 = ((bf16[384,1,1,2,128]{4,3,2,1,0:T(2,128)(2,1)}), bf16[384,1,1,2,128]{4,3,2,1,0:T(2,128)(2,1)S(1)}, u32[]{:S(2)}, u32[]{:S(2)}) async-start(bf16[384,1,1,2,128]{4,3,2,1,0:T(2,128)(2,1)} %copy.28), calls=%async_computation.1 | async-start | bytes 393216 | tf_op jit(solution)/shard_map/all_to_all | solution.py:158
  40.4 5.9 %all-to-all-done.1 = bf16[384,1,1,2,128]{4,3,2,1,0:T(2,128)(2,1)S(1)} async-done(((bf16[384,1,1,2,128]{4,3,2,1,0:T(2,128)(2,1)}), bf16[384,1,1,2,128]{4,3,2,1,0:T(2,128)(2,1)S(1)}, u32[]{:S(2)}, u32[]{:S(2)}) %all-to-all-start.1) | async-done | bytes 196640 | tf_op jit(solution)/shard_map/all_to_all | solution.py:158
  48.2 3.5 %all-to-all-start.3 = ((bf16[4,96,1,4,2,128]{5,1,4,3,2,0:T(8,128)(2,1)}), bf16[4,96,1,4,2,128]{5,1,4,3,2,0:T(8,128)(2,1)S(1)}, u32[]{:S(2)}, u32[]{:S(2)}) async-start(bf16[4,96,1,4,2,128]{5,1,4,3,2,0:T(8,128)(2,1)} %broadcast_in_dim.17), calls=%async_computation.3 | async-start | bytes 1572864 | tf_op jit(solution)/shard_map/all_to_all | solution.py:188
  51.7 4.9 %all-reduce.3 = (f32[8,1]{0,1:T(1,128)S(1)}, f32[8,1]{0,1:T(1,128)S(1)}) all-reduce(f32[8,1]{0,1:T(1,128)S(1)} %convolution_bitcast_fusion.1, f32[8,1]{0,1:T(1,128)S(1)} %convolution_bitcast_fusion), channel_id=1, replica_groups=mesh['ch'=4,'ha'=2,'dp'=4] {'ha'}, use_global_device_ids=true, to_apply=%region_10.11 | all-reduce | flops 16 | bytes 128 | tf_op jit(solution)/shard_map/psum | solution.py:161
  57.3 3.5 %collective-permute-start = (bf16[96,1,4,1,128]{4,0,3,2,1:T(8,128)(2,1)S(1)}, bf16[96,1,4,1,128]{4,0,3,2,1:T(8,128)(2,1)S(1)}, u32[]{:S(2)}, u32[]{:S(2)}) collective-permute-start(bf16[96,1,4,1,128]{4,0,3,2,1:T(8,128)(2,1)S(1)} %get-tuple-element.67), channel_id=1, source_target_pairs={{0,4},{1,5},{2,6},{3,7},{8,12},{9,13},{10,14},{11,15},{16,20},{17,... | collective-permute-start | bytes 294920 | tf_op jit(solution)/shard_map/ppermute | solution.py:19
  62.1 1.7 %fusion.117 = (bf16[1,3,3,96,384]{4,3,2,1,0:T(8,128)(2,1)S(1)}, bf16[1,3,3,96,384]{4,3,2,1,0:T(8,128)(2,1)S(1)}, bf16[1,3,3,96,384]{4,3,2,1,0:T(8,128)(2,1)S(1)}) fusion(bf16[3,3,3,96,384]{4,3,2,1,0:T(8,128)(2,1)} %param.23), kind=kLoop, calls=%fused_computation.178 | loop fusion | bytes 3981312 | tf_op jit(solution)/shard_map/slice | solution.py:171
  63.8 3.5 %collective-permute-done.1 = bf16[96,1,4,1,128]{4,0,3,2,1:T(8,128)(2,1)S(1)} collective-permute-done((bf16[96,1,4,1,128]{4,0,3,2,1:T(8,128)(2,1)S(1)}, bf16[96,1,4,1,128]{4,0,3,2,1:T(8,128)(2,1)S(1)}, u32[]{:S(2)}, u32[]{:S(2)}) %collective-permute-start.1) | collective-permute-done | bytes 98336 | tf_op jit(solution)/shard_map/ppermute | solution.py:20
  75.4 5.0 %all-to-all-start.2 = ((bf16[4,96,1,4,2,128]{5,1,4,3,2,0:T(8,128)(2,1)}), bf16[4,96,1,4,2,128]{5,1,4,3,2,0:T(8,128)(2,1)S(1)}, u32[]{:S(2)}, u32[]{:S(2)}) async-start(bf16[4,96,1,4,2,128]{5,1,4,3,2,0:T(8,128)(2,1)} %copy.32), calls=%async_computation.2 | async-start | bytes 1572864 | tf_op jit(solution)/shard_map/all_to_all | solution.py:178
  80.5 2.6 %fusion.19 = f32[1,864,384]{2,1,0:T(8,128)S(1)} fusion(bf16[384,4,2,128]{3,0,2,1:T(8,128)(2,1)S(1)} %bitcast.225, bf16[864,1,4,2,128]{4,0,3,2,1:T(8,128)(2,1)} %copy-done.6), kind=kOutput, calls=%fused_computation.29 | convolution fusion | flops 679477248 | bytes 3883008 | tf_op jit(solution)/shard_map/dot_general | solution.py:192
  83.1 2.2 %dynamic_update_slice.9 = f32[3,864,384]{2,1,0:T(8,128)} pad(f32[1,864,384]{2,1,0:T(8,128)S(1)} %fusion.19, f32[]{:T(128)} %constant.62.clone.1), padding=0_2x0_0x0_0 | pad | bytes 5308420 | tf_op jit(solution)/shard_map/dynamic_update_slice | solution.py:198
  85.3 2.2 %fusion.25 = f32[3,864,384]{2,1,0:T(8,128)} fusion(f32[3,864,384]{2,1,0:T(8,128)} %dynamic_update_slice.9, bf16[384,4,2,128]{3,0,2,1:T(8,128)(2,1)S(1)} %bitcast.226, bf16[864,1,4,2,128]{4,0,3,2,1:T(8,128)(2,1)S(1)} %copy-done.5), kind=kOutput, calls=%fused_computation.31 | convolution fusion | flops 679477248 | bytes 3883008 | tf_op jit(solution)/shard_map/dot_general | solution.py:192
  87.5 2.2 %fusion.31 = f32[3,864,384]{2,1,0:T(8,128)} fusion(f32[3,864,384]{2,1,0:T(8,128)} %fusion.25, bf16[384,4,2,128]{3,0,2,1:T(8,128)(2,1)S(1)} %bitcast.227, bf16[864,1,4,2,128]{4,0,3,2,1:T(8,128)(2,1)S(1)} %copy-done.3), kind=kOutput, calls=%fused_computation.33 | convolution fusion | flops 679477248 | bytes 3883008 | tf_op jit(solution)/shard_map/dot_general | solution.py:192
  89.6 3.9 %all-to-all-done.2 = bf16[4,96,1,4,2,128]{5,1,4,3,2,0:T(8,128)(2,1)S(1)} async-done(((bf16[4,96,1,4,2,128]{5,1,4,3,2,0:T(8,128)(2,1)}), bf16[4,96,1,4,2,128]{5,1,4,3,2,0:T(8,128)(2,1)S(1)}, u32[]{:S(2)}, u32[]{:S(2)}) %all-to-all-start.2) | async-done | bytes 786464 | tf_op jit(solution)/shard_map/all_to_all | solution.py:178
  93.5 2.4 %pad.10 = f32[2624,384]{1,0:T(8,128)S(1)} pad(f32[2592,384]{1,0:T(8,128)} %bitcast.59, f32[]{:T(128)} %constant.62.clone.1), padding=0_32x0_0 | pad | bytes 8011780 | tf_op jit(solution)/shard_map/jit(_pad)/pad | solution.py:87
  95.9 1.9 %copy-done.1 = f32[2624,384]{1,0:T(8,128)} copy-done((f32[2624,384]{1,0:T(8,128)}, f32[2624,384]{1,0:T(8,128)S(1)}, u32[]{:S(2)}) %copy-start.1) | copy-done | bytes 4030488
  98.0 2.7 %collective-permute-done.2 = bf16[1312,384]{1,0:T(8,128)(2,1)} collective-permute-done((bf16[1312,384]{1,0:T(8,128)(2,1)S(1)}, bf16[1312,384]{1,0:T(8,128)(2,1)}, u32[]{:S(2)}, u32[]{:S(2)}) %collective-permute-start.2) | collective-permute-done | bytes 1007648 | tf_op jit(solution)/shard_map/ppermute | solution.py:94
  100.7 2.0 %bitcast_add_fusion = f32[1312,384]{1,0:T(8,128)S(1)} fusion(bf16[1312,384]{1,0:T(8,128)(2,1)} %collective-permute-done.2, f32[2,1312,384]{2,1,0:T(8,128)} %bitcast.213, s32[]{:T(128)S(6)} %select_n.30), kind=kLoop, calls=%fused_computation.12 | loop fusion | flops 1007616 | bytes 5038084 | tf_op jit(solution)/shard_map/add | solution.py:95
  103.6 1.5 collective-permute-start.3
  105.1 12.3 %collective-permute-done.3 = bf16[656,384]{1,0:T(8,128)(2,1)} collective-permute-done((bf16[656,384]{1,0:T(8,128)(2,1)}, bf16[656,384]{1,0:T(8,128)(2,1)}, u32[]{:S(2)}, u32[]{:S(2)}) %collective-permute-start.3) | collective-permute-done | bytes 503840 | tf_op jit(solution)/shard_map/ppermute | solution.py:94
  117.5 2.1 %bitcast_add_fusion.1 = f32[656,384]{1,0:T(8,128)} fusion(bf16[656,384]{1,0:T(8,128)(2,1)} %collective-permute-done.3, f32[2,656,384]{2,1,0:T(8,128)S(1)} %bitcast.216, s32[]{:T(128)S(6)} %select_n.32), kind=kLoop, calls=%fused_computation.64 | loop fusion | flops 503808 | bytes 2519044 | tf_op jit(solution)/shard_map/add | solution.py:95
  120.7 7.3 %collective-permute-done.4 = bf16[328,384]{1,0:T(8,128)(2,1)S(1)} collective-permute-done((bf16[328,384]{1,0:T(8,128)(2,1)S(1)}, bf16[328,384]{1,0:T(8,128)(2,1)S(1)}, u32[]{:S(2)}, u32[]{:S(2)}) %collective-permute-start.4) | collective-permute-done | bytes 251936 | tf_op jit(solution)/shard_map/ppermute | solution.py:94
  129.4 6.1 %collective-permute-done.5 = bf16[328,384]{1,0:T(8,128)(2,1)S(1)} collective-permute-done((bf16[328,384]{1,0:T(8,128)(2,1)S(1)}, bf16[328,384]{1,0:T(8,128)(2,1)S(1)}, u32[]{:S(2)}, u32[]{:S(2)}) %collective-permute-start.5) | collective-permute-done | bytes 251936 | tf_op jit(solution)/shard_map/ppermute | solution.py:100
  135.8 1.6 %collective-permute-start.6 = (bf16[656,384]{1,0:T(8,128)(2,1)S(1)}, bf16[656,384]{1,0:T(8,128)(2,1)S(1)}, u32[]{:S(2)}, u32[]{:S(2)}) collective-permute-start(bf16[656,384]{1,0:T(8,128)(2,1)S(1)} %get-tuple-element.63), channel_id=1, source_target_pairs={{0,2},{1,3},{2,0},{3,1},{4,6},{5,7},{6,4},{7,5},{8,10},{9,11},{10,... | collective-permute-start | bytes 1511432 | tf_op jit(solution)/shard_map/ppermute | solution.py:100
  137.4 9.4 %collective-permute-done.6 = bf16[656,384]{1,0:T(8,128)(2,1)S(1)} collective-permute-done((bf16[656,384]{1,0:T(8,128)(2,1)S(1)}, bf16[656,384]{1,0:T(8,128)(2,1)S(1)}, u32[]{:S(2)}, u32[]{:S(2)}) %collective-permute-start.6) | collective-permute-done | bytes 503840 | tf_op jit(solution)/shard_map/ppermute | solution.py:100
  151.2 2.4 %convert.5 = f32[3,3,3,96,384]{4,3,2,1,0:T(8,128)} convert(bf16[3,3,3,96,384]{4,3,2,1,0:T(8,128)(2,1)S(1)} %bitcast.214) | non-fusion elementwise | flops 995328 | bytes 5971968 | tf_op jit(solution)/shard_map/reshape | solution.py:203
  (106 shorter events, 24.9 us)
Async XLA Ops:
  0.6 34.6 %copy-start = (bf16[384,384]{1,0:T(8,128)(2,1)S(1)}, bf16[384,384]{1,0:T(8,128)(2,1)}, u32[]{:S(2)}) copy-start(bf16[384,384]{1,0:T(8,128)(2,1)} %param.19) | copy-start | bytes 884740
  11.0 22.4 %slice-start = ((f32[1152]{0:T(1024)}), f32[384]{0:T(512)S(1)}, s32[]{:S(2)}) async-start(f32[1152]{0:T(1024)} %param.18), calls=%async_computation.4 | async-start | bytes 4096 | tf_op jit(solution)/shard_map/slice | solution.py:140
  11.1 11.8 %all-to-all-start = ((bf16[96,1,4,2,128]{4,0,3,1,2:T(8,128)(2,1)}), bf16[96,1,4,2,128]{4,0,3,1,2:T(8,128)(2,1)S(1)}, u32[]{:S(2)}, u32[]{:S(2)}) async-start(bf16[96,1,4,2,128]{4,0,3,1,2:T(8,128)(2,1)} %fusion.91), calls=%async_computation | async-start | bytes 393216 | tf_op jit(solution)/shard_map/all_to_all | solution.py:132
  24.5 10.8 %copy-start.12 = (f32[384]{0:T(512)S(1)}, f32[384]{0:T(512)}, u32[]{:S(2)}) copy-start(f32[384]{0:T(512)} %param.20) | copy-start | bytes 4612
  35.3 4.8 %copy-start.8 = (bf16[96,1,4,2,128]{4,3,2,1,0:T(2,128)(2,1)S(1)}, bf16[96,1,4,2,128]{4,3,2,1,0:T(2,128)(2,1)}, u32[]{:S(2)}) copy-start(bf16[96,1,4,2,128]{4,3,2,1,0:T(2,128)(2,1)} %param.25) | copy-start | bytes 589828
  35.3 11.1 %copy-start.7 = (bf16[96,1,4,2,128]{4,3,2,1,0:T(2,128)(2,1)S(1)}, bf16[96,1,4,2,128]{4,3,2,1,0:T(2,128)(2,1)}, u32[]{:S(2)}) copy-start(bf16[96,1,4,2,128]{4,3,2,1,0:T(2,128)(2,1)} %param.13) | copy-start | bytes 589828
  36.7 9.6 %all-to-all-start.1 = ((bf16[384,1,1,2,128]{4,3,2,1,0:T(2,128)(2,1)}), bf16[384,1,1,2,128]{4,3,2,1,0:T(2,128)(2,1)S(1)}, u32[]{:S(2)}, u32[]{:S(2)}) async-start(bf16[384,1,1,2,128]{4,3,2,1,0:T(2,128)(2,1)} %copy.28), calls=%async_computation.1 | async-start | bytes 393216 | tf_op jit(solution)/shard_map/all_to_all | solution.py:158
  40.4 16.6 %copy-start.9 = (f32[96]{0:T(128)S(1)}, f32[96]{0:T(128)}, u32[]{:S(2)}) copy-start(f32[96]{0:T(128)} %param.22) | copy-start | bytes 1156
  40.4 16.6 %copy-start.10 = (f32[96]{0:T(128)S(1)}, f32[96]{0:T(128)}, u32[]{:S(2)}) copy-start(f32[96]{0:T(128)} %param.21) | copy-start | bytes 1156
  48.2 27.2 %all-to-all-start.3 = ((bf16[4,96,1,4,2,128]{5,1,4,3,2,0:T(8,128)(2,1)}), bf16[4,96,1,4,2,128]{5,1,4,3,2,0:T(8,128)(2,1)S(1)}, u32[]{:S(2)}, u32[]{:S(2)}) async-start(bf16[4,96,1,4,2,128]{5,1,4,3,2,0:T(8,128)(2,1)} %broadcast_in_dim.17), calls=%async_computation.3 | async-start | bytes 1572864 | tf_op jit(solution)/shard_map/all_to_all | solution.py:188
  57.3 6.5 %collective-permute-start = (bf16[96,1,4,1,128]{4,0,3,2,1:T(8,128)(2,1)S(1)}, bf16[96,1,4,1,128]{4,0,3,2,1:T(8,128)(2,1)S(1)}, u32[]{:S(2)}, u32[]{:S(2)}) collective-permute-start(bf16[96,1,4,1,128]{4,0,3,2,1:T(8,128)(2,1)S(1)} %get-tuple-element.67), channel_id=1, source_target_pairs={{0,4},{1,5},{2,6},{3,7},{8,12},{9,13},{10,14},{11,15},{16,20},{17,... | collective-permute-start | bytes 294920 | tf_op jit(solution)/shard_map/ppermute | solution.py:19
  60.8 6.5 %collective-permute-start.1 = (bf16[96,1,4,1,128]{4,0,3,2,1:T(8,128)(2,1)S(1)}, bf16[96,1,4,1,128]{4,0,3,2,1:T(8,128)(2,1)S(1)}, u32[]{:S(2)}, u32[]{:S(2)}) collective-permute-start(bf16[96,1,4,1,128]{4,0,3,2,1:T(8,128)(2,1)S(1)} %get-tuple-element.68), channel_id=1, source_target_pairs={{4,0},{5,1},{6,2},{7,3},{12,8},{13,9},{14,10},{15,11},{20,16},{21,... | collective-permute-start | bytes 294920 | tf_op jit(solution)/shard_map/ppermute | solution.py:20
  70.0 1.5 copy-start.4
  70.0 2.7 %copy-start.6 = (bf16[864,1,4,2,128]{4,0,3,2,1:T(8,128)(2,1)}, bf16[864,1,4,2,128]{4,0,3,2,1:T(8,128)(2,1)S(1)}, u32[]{:S(2)}) copy-start(bf16[864,1,4,2,128]{4,0,3,2,1:T(8,128)(2,1)S(1)} %get-tuple-element.8) | copy-start | bytes 5308420
  70.2 2.5 %copy-start.2 = (bf16[864,1,4,2,128]{4,0,3,2,1:T(8,128)(2,1)}, bf16[864,1,4,2,128]{4,0,3,2,1:T(8,128)(2,1)S(1)}, u32[]{:S(2)}) copy-start(bf16[864,1,4,2,128]{4,0,3,2,1:T(8,128)(2,1)S(1)} %slice_dynamic-update-slice_fusion) | copy-start | bytes 5308420
  75.4 18.1 %all-to-all-start.2 = ((bf16[4,96,1,4,2,128]{5,1,4,3,2,0:T(8,128)(2,1)}), bf16[4,96,1,4,2,128]{5,1,4,3,2,0:T(8,128)(2,1)S(1)}, u32[]{:S(2)}, u32[]{:S(2)}) async-start(bf16[4,96,1,4,2,128]{5,1,4,3,2,0:T(8,128)(2,1)} %copy.32), calls=%async_computation.2 | async-start | bytes 1572864 | tf_op jit(solution)/shard_map/all_to_all | solution.py:178
  83.1 2.2 %copy-start.5 = (bf16[864,1,4,2,128]{4,0,3,2,1:T(8,128)(2,1)S(1)}, bf16[864,1,4,2,128]{4,0,3,2,1:T(8,128)(2,1)}, u32[]{:S(2)}) copy-start(bf16[864,1,4,2,128]{4,0,3,2,1:T(8,128)(2,1)} %copy-done.4) | copy-start | bytes 5308420
  85.3 2.2 %copy-start.3 = (bf16[864,1,4,2,128]{4,0,3,2,1:T(8,128)(2,1)S(1)}, bf16[864,1,4,2,128]{4,0,3,2,1:T(8,128)(2,1)}, u32[]{:S(2)}) copy-start(bf16[864,1,4,2,128]{4,0,3,2,1:T(8,128)(2,1)} %copy-done.2) | copy-start | bytes 5308420
  95.9 1.9 %copy-start.1 = (f32[2624,384]{1,0:T(8,128)}, f32[2624,384]{1,0:T(8,128)S(1)}, u32[]{:S(2)}) copy-start(f32[2624,384]{1,0:T(8,128)S(1)} %pad.10) | copy-start | bytes 12091396
  97.9 2.8 %collective-permute-start.2 = (bf16[1312,384]{1,0:T(8,128)(2,1)S(1)}, bf16[1312,384]{1,0:T(8,128)(2,1)}, u32[]{:S(2)}, u32[]{:S(2)}) collective-permute-start(bf16[1312,384]{1,0:T(8,128)(2,1)S(1)} %fusion.47), channel_id=1, source_target_pairs={{0,1},{1,0},{2,3},{3,2},{4,5},{5,4},{6,7},{7,6},{8,9},{9,8},{10,11... | collective-permute-start | bytes 3022856 | tf_op jit(solution)/shard_map/ppermute | solution.py:94
  103.6 13.8 %collective-permute-start.3 = (bf16[656,384]{1,0:T(8,128)(2,1)}, bf16[656,384]{1,0:T(8,128)(2,1)}, u32[]{:S(2)}, u32[]{:S(2)}) collective-permute-start(bf16[656,384]{1,0:T(8,128)(2,1)} %fusion.53), channel_id=1, source_target_pairs={{0,2},{1,3},{2,0},{3,1},{4,6},{5,7},{6,4},{7,5},{8,10},{9,11},{10,... | collective-permute-start | bytes 1511432 | tf_op jit(solution)/shard_map/ppermute | solution.py:94
  120.6 7.3 %collective-permute-start.4 = (bf16[328,384]{1,0:T(8,128)(2,1)S(1)}, bf16[328,384]{1,0:T(8,128)(2,1)S(1)}, u32[]{:S(2)}, u32[]{:S(2)}) collective-permute-start(bf16[328,384]{1,0:T(8,128)(2,1)S(1)} %fusion.86), channel_id=1, source_target_pairs={{0,4},{4,0},{1,5},{5,1},{2,6},{6,2},{3,7},{7,3},{8,12},{12,8},{9,1... | collective-permute-start | bytes 755720 | tf_op jit(solution)/shard_map/ppermute | solution.py:94
  129.0 6.5 %collective-permute-start.5 = (bf16[328,384]{1,0:T(8,128)(2,1)S(1)}, bf16[328,384]{1,0:T(8,128)(2,1)S(1)}, u32[]{:S(2)}, u32[]{:S(2)}) collective-permute-start(bf16[328,384]{1,0:T(8,128)(2,1)S(1)} %fusion.58), channel_id=1, source_target_pairs={{0,4},{4,0},{1,5},{5,1},{2,6},{6,2},{3,7},{7,3},{8,12},{12,8},{9,1... | collective-permute-start | bytes 755720 | tf_op jit(solution)/shard_map/ppermute | solution.py:100
  135.8 11.0 %collective-permute-start.6 = (bf16[656,384]{1,0:T(8,128)(2,1)S(1)}, bf16[656,384]{1,0:T(8,128)(2,1)S(1)}, u32[]{:S(2)}, u32[]{:S(2)}) collective-permute-start(bf16[656,384]{1,0:T(8,128)(2,1)S(1)} %get-tuple-element.63), channel_id=1, source_target_pairs={{0,2},{1,3},{2,0},{3,1},{4,6},{5,7},{6,4},{7,5},{8,10},{9,11},{10,... | collective-permute-start | bytes 1511432 | tf_op jit(solution)/shard_map/ppermute | solution.py:100
  147.3 0.7 copy-start.11
  147.5 2.7 %collective-permute-start.7 = (bf16[1312,384]{1,0:T(8,128)(2,1)S(1)}, bf16[1312,384]{1,0:T(8,128)(2,1)S(1)}, u32[]{:S(2)}, u32[]{:S(2)}) collective-permute-start(bf16[1312,384]{1,0:T(8,128)(2,1)S(1)} %get-tuple-element.59), channel_id=1, source_target_pairs={{0,1},{1,0},{2,3},{3,2},{4,5},{5,4},{6,7},{7,6},{8,9},{9,8},{10,11... | collective-permute-start | bytes 3022856 | tf_op jit(solution)/shard_map/ppermute | solution.py:100

commit v6 on v4

--- a/solution.py
+++ b/solution.py
@@ -105,6 +105,15 @@
     return work[:length].astype(jnp.float32)
 
 
+def doubling_sum(values, axis):
+    size = lax.axis_size(axis)
+    for bit in range(size.bit_length() - 1):
+        perm = [(i, i ^ (1 << bit)) for i in range(size)]
+        got = lax.ppermute(values, axis, perm)
+        values = tuple(a + b for a, b in zip(values, got))
+    return values
+
+
 def body(
     features,
     frame_count,
@@ -125,7 +134,7 @@
     mask = frame_mask(frame_count, frames)
     count = frame_count.astype(jnp.float32) * (chans // groups * rows * lax.axis_size("ha") * cols)
     first, second = moments(features, mask, groups)
-    first, second = lax.psum((first, second), "ha")
+    first, second = doubling_sum((first, second), "ha")
     normed = normalize(features, first, second, count, norm1_gain, norm1_shift, groups).astype(
         jnp.bfloat16
     )
@@ -158,7 +167,7 @@
     update = lax.all_to_all(projected, "ch", split_axis=0, concat_axis=2, tiled=True)
     hidden = (features.astype(jnp.float32) + update.astype(jnp.float32)).astype(jnp.bfloat16)
     first, second = moments(hidden, mask, groups)
-    first, second = lax.psum((first, second), "ha")
+    first, second = doubling_sum((first, second), "ha")
     gated = jax.nn.silu(
         normalize(hidden, first, second, count, norm2_gain, norm2_shift, groups)
     ).astype(jnp.bfloat16)

time: 154 us -> 153 us (level)
  blocking collectives: 19.7 us -> 8.66 us
  waiting for transfers between devices: 57.1 us -> 62.7 us
  starting transfers between devices: 26.1 us -> 30.6 us
    psum x2 -> x0, blocking collectives: 10.8 us -> none  [body(): first, second = lax.psum((first, second), 'ha')]
    ppermute x0 -> x4, waiting for transfers between devices: none -> 5.65 us  [doubling_sum(): got = lax.ppermute(values, axis, perm)]
    ppermute x0 -> x4, starting transfers between devices: none -> 5.03 us  [doubling_sum(): got = lax.ppermute(values, axis, perm)]
  transfers between devices with their start and end apart: 12 -> 16, of which waited for: 9 -> 13; matrix products, arithmetic and copies ran while one was open for 10% -> 11% of each run, Pallas kernels for 0% -> 0%
where the time goes in v6:
time: 153 us; the launch traced here: 152 us
  waiting for transfers between devices  62.7 us (41%)
  starting transfers between devices  30.6 us (20%)
  other arithmetic  19.2 us (13%)
  local copies, waits for them, and re-layouts  16.6 us (11%)
  matrix products  12.6 us (8%)
  blocking collectives  8.66 us (6%)
  between operations  1.87 us (1%)
    ppermute x3, waiting for transfers between devices, butterfly_sum(): got = lax.ppermute(send.astype(jnp.bfloat16), axis, perm)  22.1 us
    all_to_all x1, waiting for transfers between devices, body(): parts = lax.all_to_all(parts, 'ch', split_axis=0, concat_axis=0, tiled=True)  11.7 us
    ppermute x3, waiting for transfers between devices, butterfly_sum(): got = lax.ppermute(work, axis, perm)  9.43 us
    all_gather x1, blocking collectives, body(): piece = lax.all_gather(pairs, 'ha', axis=1, tiled=True)  8.66 us
    unnamed x39, local copies, waits for them, and re-layouts  5.97 us
    all_to_all x1, waiting for transfers between devices, body(): lax.all_to_all(projected, 'ch', split_axis=0, concat_axis=2, tiled=True)  5.88 us
    ppermute x4, waiting for transfers between devices, doubling_sum(): got = lax.ppermute(values, axis, perm)  5.65 us
    all_to_all x1, waiting for transfers between devices, body(): lax.all_to_all(normed, 'ch', split_axis=2, concat_axis=0, tiled=True)  5.55 us
  transfers between devices with their start and end apart: 16, of which 13 were waited for; matrix products, arithmetic and copies ran while one was open for 11% of the time, Pallas kernels for 0%

profile of v6, /device:TPU:0, one launch (start us, length us, event | category | flops | bytes accessed | tf_op | source)
XLA Modules:
  0.0 152.2 jit_solution(14878665267219705704)
XLA Ops:
  2.8 3.0 %collective-permute-start = (f32[8,1]{0,1:T(1,128)S(1)}, f32[8,1]{0,1:T(1,128)S(1)}, u32[]{:S(2)}, u32[]{:S(2)}) collective-permute-start(f32[8,1]{0,1:T(1,128)S(1)} %convolution_bitcast_fusion.3), channel_id=1, source_target_pairs={{0,4},{4,0},{1,5},{5,1},{2,6},{6,2},{3,7},{7,3},{8,12},{12,8},{9,1... | collective-permute-start | bytes 104 | tf_op jit(solution)/shard_map/ppermute | solution.py:112
  7.3 2.3 %collective-permute-done.1 = f32[8,1]{0,1:T(1,128)S(1)} collective-permute-done((f32[8,1]{0,1:T(1,128)S(1)}, f32[8,1]{0,1:T(1,128)S(1)}, u32[]{:S(2)}, u32[]{:S(2)}) %collective-permute-start.1) | collective-permute-done | bytes 64 | tf_op jit(solution)/shard_map/ppermute | solution.py:112
  9.9 1.8 %fusion.91 = bf16[96,1,4,2,128]{4,0,3,1,2:T(8,128)(2,1)} fusion(f32[96]{0:T(128)} %param.16, f32[96]{0:T(128)} %param.15, f32[96]{0:T(128)S(1)} %mul.117, f32[96]{0:T(128)S(1)} %sub.78, bf16[96,1,4,2,128]{4,3,2,1,0:T(2,128)(2,1)} %param.13), kind=kLoop, calls=%fused_computation.119 | loop fusion | flops 589824 | bytes 394752 | tf_op jit(solution)/shard_map/convert_element_type | solution.py:138
  11.8 5.0 %all-to-all-start = ((bf16[96,1,4,2,128]{4,0,3,1,2:T(8,128)(2,1)}), bf16[96,1,4,2,128]{4,0,3,1,2:T(8,128)(2,1)S(1)}, u32[]{:S(2)}, u32[]{:S(2)}) async-start(bf16[96,1,4,2,128]{4,0,3,1,2:T(8,128)(2,1)} %fusion.91), calls=%async_computation | async-start | bytes 393216 | tf_op jit(solution)/shard_map/all_to_all | solution.py:141
  17.5 5.5 %all-to-all-done = bf16[96,1,4,2,128]{4,0,3,1,2:T(8,128)(2,1)S(1)} async-done(((bf16[96,1,4,2,128]{4,0,3,1,2:T(8,128)(2,1)}), bf16[96,1,4,2,128]{4,0,3,1,2:T(8,128)(2,1)S(1)}, u32[]{:S(2)}, u32[]{:S(2)}) %all-to-all-start) | async-done | bytes 196640 | tf_op jit(solution)/shard_map/all_to_all | solution.py:141
  23.2 1.5 fusion.37
  24.6 8.7 %all-gather = bf16[512,768]{1,0:T(8,128)(2,1)S(1)} all-gather(bf16[256,768]{1,0:T(8,128)(2,1)S(1)} %fusion.37), channel_id=2, replica_groups=mesh['ch'=4,'ha'=2,'dp'=4] {'ha'}, dimensions={0}, use_global_device_ids=true | all-gather | bytes 1179648 | tf_op jit(solution)/shard_map/all_gather | solution.py:160
  33.3 1.6 %fusion.119 = (f32[256]{0:T(256)S(1)}, f32[256,512]{1,0:T(8,128)S(1)}) fusion(bf16[1,512,768]{2,1,0:T(8,128)(2,1)S(1)} %bitcast.223, bf16[384,1152]{1,0:T(8,128)(2,1)} %param.17, f32[384]{0:T(512)S(1)} %slice-done, bf16[48,8,2,128]{3,2,1,0:T(2,128)(2,1)S(1)} %bitcast.232), kind=kOutput, calls=%fused_computation.180 | convolution fusion | flops 176619264 | bytes 1412096 | tf_op jit(solution)/shard_map/itc,isc->its/dot_general | solution.py:51
  36.6 3.4 %all-to-all-start.1 = ((bf16[384,1,1,2,128]{4,3,2,1,0:T(2,128)(2,1)}), bf16[384,1,1,2,128]{4,3,2,1,0:T(2,128)(2,1)S(1)}, u32[]{:S(2)}, u32[]{:S(2)}) async-start(bf16[384,1,1,2,128]{4,3,2,1,0:T(2,128)(2,1)} %copy.28), calls=%async_computation.1 | async-start | bytes 393216 | tf_op jit(solution)/shard_map/all_to_all | solution.py:167
  40.3 5.9 %all-to-all-done.1 = bf16[384,1,1,2,128]{4,3,2,1,0:T(2,128)(2,1)S(1)} async-done(((bf16[384,1,1,2,128]{4,3,2,1,0:T(2,128)(2,1)}), bf16[384,1,1,2,128]{4,3,2,1,0:T(2,128)(2,1)S(1)}, u32[]{:S(2)}, u32[]{:S(2)}) %all-to-all-start.1) | async-done | bytes 196640 | tf_op jit(solution)/shard_map/all_to_all | solution.py:167
  47.2 3.5 %all-to-all-start.3 = ((bf16[4,96,1,4,2,128]{5,1,4,3,2,0:T(8,128)(2,1)}), bf16[4,96,1,4,2,128]{5,1,4,3,2,0:T(8,128)(2,1)S(1)}, u32[]{:S(2)}, u32[]{:S(2)}) async-start(bf16[4,96,1,4,2,128]{5,1,4,3,2,0:T(8,128)(2,1)} %broadcast_in_dim.17), calls=%async_computation.3 | async-start | bytes 1572864 | tf_op jit(solution)/shard_map/all_to_all | solution.py:197
  52.1 1.5 collective-permute-start.3
  56.4 3.4 %collective-permute-start.4 = (bf16[96,1,4,1,128]{4,0,3,2,1:T(8,128)(2,1)S(1)}, bf16[96,1,4,1,128]{4,0,3,2,1:T(8,128)(2,1)S(1)}, u32[]{:S(2)}, u32[]{:S(2)}) collective-permute-start(bf16[96,1,4,1,128]{4,0,3,2,1:T(8,128)(2,1)S(1)} %get-tuple-element.61), channel_id=1, source_target_pairs={{0,4},{1,5},{2,6},{3,7},{8,12},{9,13},{10,14},{11,15},{16,20},{17,... | collective-permute-start | bytes 294920 | tf_op jit(solution)/shard_map/ppermute | solution.py:19
  59.8 1.5 collective-permute-start.5
  61.3 2.6 %fusion.117 = (bf16[1,3,3,96,384]{4,3,2,1,0:T(8,128)(2,1)}, bf16[1,3,3,96,384]{4,3,2,1,0:T(8,128)(2,1)S(1)}, bf16[1,3,3,96,384]{4,3,2,1,0:T(8,128)(2,1)S(1)}) fusion(bf16[3,3,3,96,384]{4,3,2,1,0:T(8,128)(2,1)} %param.23), kind=kLoop, calls=%fused_computation.178 | loop fusion | bytes 3981312 | tf_op jit(solution)/shard_map/slice | solution.py:180
  63.9 2.5 %collective-permute-done.5 = bf16[96,1,4,1,128]{4,0,3,2,1:T(8,128)(2,1)S(1)} collective-permute-done((bf16[96,1,4,1,128]{4,0,3,2,1:T(8,128)(2,1)S(1)}, bf16[96,1,4,1,128]{4,0,3,2,1:T(8,128)(2,1)S(1)}, u32[]{:S(2)}, u32[]{:S(2)}) %collective-permute-start.5) | collective-permute-done | bytes 98336 | tf_op jit(solution)/shard_map/ppermute | solution.py:20
  73.1 2.6 %fusion.19 = f32[1,864,384]{2,1,0:T(8,128)S(1)} fusion(bf16[384,4,2,128]{3,0,2,1:T(8,128)(2,1)S(1)} %bitcast.225, bf16[864,1,4,2,128]{4,0,3,2,1:T(8,128)(2,1)} %copy-done.7), kind=kOutput, calls=%fused_computation.29 | convolution fusion | flops 679477248 | bytes 3883008 | tf_op jit(solution)/shard_map/dot_general | solution.py:201
  80.1 1.9 %copy-done.1 = f32[2624,384]{1,0:T(8,128)} copy-done((f32[2624,384]{1,0:T(8,128)}, f32[2624,384]{1,0:T(8,128)S(1)}, u32[]{:S(2)}) %copy-start.1) | copy-done | bytes 4030488
  82.2 2.7 %collective-permute-done.6 = bf16[1312,384]{1,0:T(8,128)(2,1)} collective-permute-done((bf16[1312,384]{1,0:T(8,128)(2,1)S(1)}, bf16[1312,384]{1,0:T(8,128)(2,1)}, u32[]{:S(2)}, u32[]{:S(2)}) %collective-permute-start.6) | collective-permute-done | bytes 1007648 | tf_op jit(solution)/shard_map/ppermute | solution.py:94
  84.9 2.0 %bitcast_add_fusion = f32[1312,384]{1,0:T(8,128)S(1)} fusion(bf16[1312,384]{1,0:T(8,128)(2,1)} %collective-permute-done.6, f32[2,1312,384]{2,1,0:T(8,128)} %bitcast.214, s32[]{:T(128)S(6)} %select_n.30), kind=kLoop, calls=%fused_computation.12 | loop fusion | flops 1007616 | bytes 5038084 | tf_op jit(solution)/shard_map/add | solution.py:95
  87.8 1.5 %collective-permute-start.7 = (bf16[656,384]{1,0:T(8,128)(2,1)}, bf16[656,384]{1,0:T(8,128)(2,1)}, u32[]{:S(2)}, u32[]{:S(2)}) collective-permute-start(bf16[656,384]{1,0:T(8,128)(2,1)} %fusion.53), channel_id=1, source_target_pairs={{0,2},{1,3},{2,0},{3,1},{4,6},{5,7},{6,4},{7,5},{8,10},{9,11},{10,... | collective-permute-start | bytes 1511432 | tf_op jit(solution)/shard_map/ppermute | solution.py:94
  89.3 12.3 %collective-permute-done.7 = bf16[656,384]{1,0:T(8,128)(2,1)} collective-permute-done((bf16[656,384]{1,0:T(8,128)(2,1)}, bf16[656,384]{1,0:T(8,128)(2,1)}, u32[]{:S(2)}, u32[]{:S(2)}) %collective-permute-start.7) | collective-permute-done | bytes 503840 | tf_op jit(solution)/shard_map/ppermute | solution.py:94
  101.6 2.1 %bitcast_add_fusion.1 = f32[656,384]{1,0:T(8,128)} fusion(bf16[656,384]{1,0:T(8,128)(2,1)} %collective-permute-done.7, f32[2,656,384]{2,1,0:T(8,128)S(1)} %bitcast.217, s32[]{:T(128)S(6)} %select_n.32), kind=kLoop, calls=%fused_computation.64 | loop fusion | flops 503808 | bytes 2519044 | tf_op jit(solution)/shard_map/add | solution.py:95
  105.0 7.1 %collective-permute-done.8 = bf16[328,384]{1,0:T(8,128)(2,1)S(1)} collective-permute-done((bf16[328,384]{1,0:T(8,128)(2,1)S(1)}, bf16[328,384]{1,0:T(8,128)(2,1)S(1)}, u32[]{:S(2)}, u32[]{:S(2)}) %collective-permute-start.8) | collective-permute-done | bytes 251936 | tf_op jit(solution)/shard_map/ppermute | solution.py:94
  113.5 6.1 %collective-permute-done.9 = bf16[328,384]{1,0:T(8,128)(2,1)S(1)} collective-permute-done((bf16[328,384]{1,0:T(8,128)(2,1)S(1)}, bf16[328,384]{1,0:T(8,128)(2,1)S(1)}, u32[]{:S(2)}, u32[]{:S(2)}) %collective-permute-start.9) | collective-permute-done | bytes 251936 | tf_op jit(solution)/shard_map/ppermute | solution.py:100
  120.9 1.5 %collective-permute-start.10 = (bf16[656,384]{1,0:T(8,128)(2,1)}, bf16[656,384]{1,0:T(8,128)(2,1)}, u32[]{:S(2)}, u32[]{:S(2)}) collective-permute-start(bf16[656,384]{1,0:T(8,128)(2,1)} %get-tuple-element.57), channel_id=1, source_target_pairs={{0,2},{1,3},{2,0},{3,1},{4,6},{5,7},{6,4},{7,5},{8,10},{9,11},{10,... | collective-permute-start | bytes 1511432 | tf_op jit(solution)/shard_map/ppermute | solution.py:100
  123.9 5.1 %all-to-all-start.2 = ((bf16[4,96,1,4,2,128]{5,1,4,3,2,0:T(8,128)(2,1)}), bf16[4,96,1,4,2,128]{5,1,4,3,2,0:T(8,128)(2,1)S(1)}, u32[]{:S(2)}, u32[]{:S(2)}) async-start(bf16[4,96,1,4,2,128]{5,1,4,3,2,0:T(8,128)(2,1)} %copy.32), calls=%async_computation.2 | async-start | bytes 1572864 | tf_op jit(solution)/shard_map/all_to_all | solution.py:187
  128.9 3.3 %collective-permute-done.10 = bf16[656,384]{1,0:T(8,128)(2,1)} collective-permute-done((bf16[656,384]{1,0:T(8,128)(2,1)}, bf16[656,384]{1,0:T(8,128)(2,1)}, u32[]{:S(2)}, u32[]{:S(2)}) %collective-permute-start.10) | collective-permute-done | bytes 503840 | tf_op jit(solution)/shard_map/ppermute | solution.py:100
  132.2 1.5 fusion.57
  134.8 11.7 %all-to-all-done.2 = bf16[4,96,1,4,2,128]{5,1,4,3,2,0:T(8,128)(2,1)S(1)} async-done(((bf16[4,96,1,4,2,128]{5,1,4,3,2,0:T(8,128)(2,1)}), bf16[4,96,1,4,2,128]{5,1,4,3,2,0:T(8,128)(2,1)S(1)}, u32[]{:S(2)}, u32[]{:S(2)}) %all-to-all-start.2) | async-done | bytes 786464 | tf_op jit(solution)/shard_map/all_to_all | solution.py:187
  147.6 2.0 %fusion.51 = (bf16[1312,384]{1,0:T(8,128)(2,1)S(1)}, bf16[1312,384]{1,0:T(8,128)(2,1)S(1)}) fusion(s32[]{:T(128)S(6)} %select_n.30, bf16[1,1312,384]{2,1,0:T(8,128)(2,1)S(1)} %get-tuple-element.54, bf16[1,1312,384]{2,1,0:T(8,128)(2,1)} %bitcast.78, s32[]{:T(128)S(6)} %select_n.31), kind=kLoop, calls=%fused_computation.62 | loop fusion | flops 1007616 | bytes 4030472 | tf_op jit(solution)/shard_map/jit(dynamic_index_in_dim)/squeeze | solution.py:102
  149.8 2.4 %convert.5 = f32[3,3,3,96,384]{4,3,2,1,0:T(8,128)} convert(bf16[3,3,3,96,384]{4,3,2,1,0:T(8,128)(2,1)S(1)} %bitcast.215) | non-fusion elementwise | flops 995328 | bytes 5971968 | tf_op jit(solution)/shard_map/reshape | solution.py:211
  (116 shorter events, 31.0 us)
Async XLA Ops:
  0.6 34.5 %copy-start = (bf16[384,384]{1,0:T(8,128)(2,1)S(1)}, bf16[384,384]{1,0:T(8,128)(2,1)}, u32[]{:S(2)}) copy-start(bf16[384,384]{1,0:T(8,128)(2,1)} %param.19) | copy-start | bytes 884740
  2.8 4.5 %collective-permute-start = (f32[8,1]{0,1:T(1,128)S(1)}, f32[8,1]{0,1:T(1,128)S(1)}, u32[]{:S(2)}, u32[]{:S(2)}) collective-permute-start(f32[8,1]{0,1:T(1,128)S(1)} %convolution_bitcast_fusion.3), channel_id=1, source_target_pairs={{0,4},{4,0},{1,5},{5,1},{2,6},{6,2},{3,7},{7,3},{8,12},{12,8},{9,1... | collective-permute-start | bytes 104 | tf_op jit(solution)/shard_map/ppermute | solution.py:112
  6.0 3.6 %collective-permute-start.1 = (f32[8,1]{0,1:T(1,128)S(1)}, f32[8,1]{0,1:T(1,128)S(1)}, u32[]{:S(2)}, u32[]{:S(2)}) collective-permute-start(f32[8,1]{0,1:T(1,128)S(1)} %convolution_bitcast_fusion.2), channel_id=1, source_target_pairs={{0,4},{4,0},{1,5},{5,1},{2,6},{6,2},{3,7},{7,3},{8,12},{12,8},{9,1... | collective-permute-start | bytes 104 | tf_op jit(solution)/shard_map/ppermute | solution.py:112
  11.8 21.5 %slice-start = ((f32[1152]{0:T(1024)}), f32[384]{0:T(512)S(1)}, s32[]{:S(2)}) async-start(f32[1152]{0:T(1024)} %param.18), calls=%async_computation.4 | async-start | bytes 4096 | tf_op jit(solution)/shard_map/slice | solution.py:149
  11.8 11.3 %all-to-all-start = ((bf16[96,1,4,2,128]{4,0,3,1,2:T(8,128)(2,1)}), bf16[96,1,4,2,128]{4,0,3,1,2:T(8,128)(2,1)S(1)}, u32[]{:S(2)}, u32[]{:S(2)}) async-start(bf16[96,1,4,2,128]{4,0,3,1,2:T(8,128)(2,1)} %fusion.91), calls=%async_computation | async-start | bytes 393216 | tf_op jit(solution)/shard_map/all_to_all | solution.py:141
  24.6 10.5 %copy-start.14 = (f32[384]{0:T(512)S(1)}, f32[384]{0:T(512)}, u32[]{:S(2)}) copy-start(f32[384]{0:T(512)} %param.20) | copy-start | bytes 4612
  35.2 4.8 %copy-start.10 = (bf16[96,1,4,2,128]{4,3,2,1,0:T(2,128)(2,1)S(1)}, bf16[96,1,4,2,128]{4,3,2,1,0:T(2,128)(2,1)}, u32[]{:S(2)}) copy-start(bf16[96,1,4,2,128]{4,3,2,1,0:T(2,128)(2,1)} %param.25) | copy-start | bytes 589828
  36.6 9.6 %all-to-all-start.1 = ((bf16[384,1,1,2,128]{4,3,2,1,0:T(2,128)(2,1)}), bf16[384,1,1,2,128]{4,3,2,1,0:T(2,128)(2,1)S(1)}, u32[]{:S(2)}, u32[]{:S(2)}) async-start(bf16[384,1,1,2,128]{4,3,2,1,0:T(2,128)(2,1)} %copy.28), calls=%async_computation.1 | async-start | bytes 393216 | tf_op jit(solution)/shard_map/all_to_all | solution.py:167
  40.2 10.5 %copy-start.9 = (bf16[96,1,4,2,128]{4,3,2,1,0:T(2,128)(2,1)S(1)}, bf16[96,1,4,2,128]{4,3,2,1,0:T(2,128)(2,1)}, u32[]{:S(2)}) copy-start(bf16[96,1,4,2,128]{4,3,2,1,0:T(2,128)(2,1)} %param.13) | copy-start | bytes 589828
  40.3 15.8 %copy-start.11 = (f32[96]{0:T(128)S(1)}, f32[96]{0:T(128)}, u32[]{:S(2)}) copy-start(f32[96]{0:T(128)} %param.22) | copy-start | bytes 1156
  40.3 15.7 %copy-start.12 = (f32[96]{0:T(128)S(1)}, f32[96]{0:T(128)}, u32[]{:S(2)}) copy-start(f32[96]{0:T(128)} %param.21) | copy-start | bytes 1156
  47.2 25.8 %all-to-all-start.3 = ((bf16[4,96,1,4,2,128]{5,1,4,3,2,0:T(8,128)(2,1)}), bf16[4,96,1,4,2,128]{5,1,4,3,2,0:T(8,128)(2,1)S(1)}, u32[]{:S(2)}, u32[]{:S(2)}) async-start(bf16[4,96,1,4,2,128]{5,1,4,3,2,0:T(8,128)(2,1)} %broadcast_in_dim.17), calls=%async_computation.3 | async-start | bytes 1572864 | tf_op jit(solution)/shard_map/all_to_all | solution.py:197
  51.3 3.6 %collective-permute-start.2 = (f32[8,1]{0,1:T(1,128)S(1)}, f32[8,1]{0,1:T(1,128)S(1)}, u32[]{:S(2)}, u32[]{:S(2)}) collective-permute-start(f32[8,1]{0,1:T(1,128)S(1)} %convolution_bitcast_fusion.1), channel_id=1, source_target_pairs={{0,4},{4,0},{1,5},{5,1},{2,6},{6,2},{3,7},{7,3},{8,12},{12,8},{9,1... | collective-permute-start | bytes 104 | tf_op jit(solution)/shard_map/ppermute | solution.py:112
  52.1 3.6 %collective-permute-start.3 = (f32[8,1]{0,1:T(1,128)S(1)}, f32[8,1]{0,1:T(1,128)S(1)}, u32[]{:S(2)}, u32[]{:S(2)}) collective-permute-start(f32[8,1]{0,1:T(1,128)S(1)} %convolution_bitcast_fusion), channel_id=1, source_target_pairs={{0,4},{4,0},{1,5},{5,1},{2,6},{6,2},{3,7},{7,3},{8,12},{12,8},{9,1... | collective-permute-start | bytes 104 | tf_op jit(solution)/shard_map/ppermute | solution.py:112
  56.4 7.5 %collective-permute-start.4 = (bf16[96,1,4,1,128]{4,0,3,2,1:T(8,128)(2,1)S(1)}, bf16[96,1,4,1,128]{4,0,3,2,1:T(8,128)(2,1)S(1)}, u32[]{:S(2)}, u32[]{:S(2)}) collective-permute-start(bf16[96,1,4,1,128]{4,0,3,2,1:T(8,128)(2,1)S(1)} %get-tuple-element.61), channel_id=1, source_target_pairs={{0,4},{1,5},{2,6},{3,7},{8,12},{9,13},{10,14},{11,15},{16,20},{17,... | collective-permute-start | bytes 294920 | tf_op jit(solution)/shard_map/ppermute | solution.py:19
  59.8 6.5 %collective-permute-start.5 = (bf16[96,1,4,1,128]{4,0,3,2,1:T(8,128)(2,1)S(1)}, bf16[96,1,4,1,128]{4,0,3,2,1:T(8,128)(2,1)S(1)}, u32[]{:S(2)}, u32[]{:S(2)}) collective-permute-start(bf16[96,1,4,1,128]{4,0,3,2,1:T(8,128)(2,1)S(1)} %get-tuple-element.62), channel_id=1, source_target_pairs={{4,0},{5,1},{6,2},{7,3},{12,8},{13,9},{14,10},{15,11},{20,16},{21,... | collective-permute-start | bytes 294920 | tf_op jit(solution)/shard_map/ppermute | solution.py:20
  68.1 1.2 copy-start.2
  69.1 1.5 copy-start.5
  69.1 2.7 %copy-start.7 = (bf16[864,1,4,2,128]{4,0,3,2,1:T(8,128)(2,1)}, bf16[864,1,4,2,128]{4,0,3,2,1:T(8,128)(2,1)S(1)}, u32[]{:S(2)}) copy-start(bf16[864,1,4,2,128]{4,0,3,2,1:T(8,128)(2,1)S(1)} %get-tuple-element.7) | copy-start | bytes 5308420
  69.3 2.5 %copy-start.3 = (bf16[864,1,4,2,128]{4,0,3,2,1:T(8,128)(2,1)}, bf16[864,1,4,2,128]{4,0,3,2,1:T(8,128)(2,1)S(1)}, u32[]{:S(2)}) copy-start(bf16[864,1,4,2,128]{4,0,3,2,1:T(8,128)(2,1)S(1)} %slice_dynamic-update-slice_fusion) | copy-start | bytes 5308420
  75.7 1.5 copy-start.6
  77.2 1.5 copy-start.4
  80.0 1.9 %copy-start.1 = (f32[2624,384]{1,0:T(8,128)}, f32[2624,384]{1,0:T(8,128)S(1)}, u32[]{:S(2)}) copy-start(f32[2624,384]{1,0:T(8,128)S(1)} %pad.10) | copy-start | bytes 12091396
  82.1 2.8 %collective-permute-start.6 = (bf16[1312,384]{1,0:T(8,128)(2,1)S(1)}, bf16[1312,384]{1,0:T(8,128)(2,1)}, u32[]{:S(2)}, u32[]{:S(2)}) collective-permute-start(bf16[1312,384]{1,0:T(8,128)(2,1)S(1)} %fusion.47), channel_id=1, source_target_pairs={{0,1},{1,0},{2,3},{3,2},{4,5},{5,4},{6,7},{7,6},{8,9},{9,8},{10,11... | collective-permute-start | bytes 3022856 | tf_op jit(solution)/shard_map/ppermute | solution.py:94
  87.8 13.8 %collective-permute-start.7 = (bf16[656,384]{1,0:T(8,128)(2,1)}, bf16[656,384]{1,0:T(8,128)(2,1)}, u32[]{:S(2)}, u32[]{:S(2)}) collective-permute-start(bf16[656,384]{1,0:T(8,128)(2,1)} %fusion.53), channel_id=1, source_target_pairs={{0,2},{1,3},{2,0},{3,1},{4,6},{5,7},{6,4},{7,5},{8,10},{9,11},{10,... | collective-permute-start | bytes 1511432 | tf_op jit(solution)/shard_map/ppermute | solution.py:94
  104.8 7.3 %collective-permute-start.8 = (bf16[328,384]{1,0:T(8,128)(2,1)S(1)}, bf16[328,384]{1,0:T(8,128)(2,1)S(1)}, u32[]{:S(2)}, u32[]{:S(2)}) collective-permute-start(bf16[328,384]{1,0:T(8,128)(2,1)S(1)} %fusion.86), channel_id=1, source_target_pairs={{0,4},{4,0},{1,5},{5,1},{2,6},{6,2},{3,7},{7,3},{8,12},{12,8},{9,1... | collective-permute-start | bytes 755720 | tf_op jit(solution)/shard_map/ppermute | solution.py:94
  113.2 6.5 %collective-permute-start.9 = (bf16[328,384]{1,0:T(8,128)(2,1)S(1)}, bf16[328,384]{1,0:T(8,128)(2,1)S(1)}, u32[]{:S(2)}, u32[]{:S(2)}) collective-permute-start(bf16[328,384]{1,0:T(8,128)(2,1)S(1)} %fusion.58), channel_id=1, source_target_pairs={{0,4},{4,0},{1,5},{5,1},{2,6},{6,2},{3,7},{7,3},{8,12},{12,8},{9,1... | collective-permute-start | bytes 755720 | tf_op jit(solution)/shard_map/ppermute | solution.py:100
  120.9 11.3 %collective-permute-start.10 = (bf16[656,384]{1,0:T(8,128)(2,1)}, bf16[656,384]{1,0:T(8,128)(2,1)}, u32[]{:S(2)}, u32[]{:S(2)}) collective-permute-start(bf16[656,384]{1,0:T(8,128)(2,1)} %get-tuple-element.57), channel_id=1, source_target_pairs={{0,2},{1,3},{2,0},{3,1},{4,6},{5,7},{6,4},{7,5},{8,10},{9,11},{10,... | collective-permute-start | bytes 1511432 | tf_op jit(solution)/shard_map/ppermute | solution.py:100
  122.9 9.3 %copy-start.8 = (bf16[1,656,384]{2,1,0:T(8,128)(2,1)S(1)}, bf16[1,656,384]{2,1,0:T(8,128)(2,1)}, u32[]{:S(2)}) copy-start(bf16[1,656,384]{2,1,0:T(8,128)(2,1)} %get-tuple-element.58) | copy-start | bytes 1511428
  123.9 22.6 %all-to-all-start.2 = ((bf16[4,96,1,4,2,128]{5,1,4,3,2,0:T(8,128)(2,1)}), bf16[4,96,1,4,2,128]{5,1,4,3,2,0:T(8,128)(2,1)S(1)}, u32[]{:S(2)}, u32[]{:S(2)}) async-start(bf16[4,96,1,4,2,128]{5,1,4,3,2,0:T(8,128)(2,1)} %copy.32), calls=%async_computation.2 | async-start | bytes 1572864 | tf_op jit(solution)/shard_map/all_to_all | solution.py:187
  133.7 12.9 %copy-start.13 = (f32[96]{0:T(128)S(1)}, f32[96]{0:T(128)}, u32[]{:S(2)}) copy-start(f32[96]{0:T(128)} %param.24) | copy-start | bytes 1156
  134.8 12.8 %collective-permute-start.11 = (bf16[1312,384]{1,0:T(8,128)(2,1)}, bf16[1312,384]{1,0:T(8,128)(2,1)}, u32[]{:S(2)}, u32[]{:S(2)}) collective-permute-start(bf16[1312,384]{1,0:T(8,128)(2,1)} %get-tuple-element.53), channel_id=1, source_target_pairs={{0,1},{1,0},{2,3},{3,2},{4,5},{5,4},{6,7},{7,6},{8,9},{9,8},{10,11... | collective-permute-start | bytes 3022856 | tf_op jit(solution)/shard_map/ppermute | solution.py:100
